TPU v7x, 256 devices: a whole 4x4x8 slice. The times are simulated.
256 devices in a mesh: video: 4 (over x), tm: 16 (over z, core), space: 4 (over y).
Axes of the slice: x: 4, y: 4, z: 8, core: 2. Of those that a mesh axis runs over, the one named last changes fastest.
Arguments:
- feature_maps: bfloat16 [64, 128, 240, 128], P(('video', 'tm'), 'space'), parts along dimension 0, may hold values from -27 to 27
- query_frame: int32 [2048], P('video'), parts along dimension 0, may hold values from 0 to 15
- query_row: int32 [2048], P('video'), parts along dimension 0, may hold values from 0 to 127
- query_col: int32 [2048], P('video'), parts along dimension 0, may hold values from 0 to 239
- ema_decay: float32 [64, 128], P(('video', 'tm')), parts along dimension 0, may hold values from 0.14 to 1
- dw_kernel: float32 [3, 128], replicated, may hold values from -3 to 3
- pw_weight: bfloat16 [128, 128], replicated, may hold values from -0.5 to 0.5
- out_weight: float32 [2, 128], replicated, may hold values from -2 to 2
Outputs:
- tracks: float32 [64, 2, 512], P(('video', 'tm')), parts along dimension 0
There are 4 independent parts, one for each index of `video`. A program takes and returns all parts, laid end to end along the dimension named above; an argument that names none is the same for every part. Nothing has to cross between parts.
All inputs are finite; a program needn't handle non-finite values.
Results may differ from a plain program's by a relative error of at most 0.0026.
Values may be sent and summed in bfloat16 or wider, within the bound.
A program may use at most 128 MiB of HBM per device.

v0:
```python
import math

import jax
import jax.numpy as jnp
from jax import lax
from jax.sharding import PartitionSpec as P


def with_halo(cells, sides, width):
    for axis, dim in sides:
        count = lax.axis_size(axis)
        ends = count - 1
        head = lax.slice_in_dim(cells, 0, width, axis=dim)
        tail = lax.slice_in_dim(cells, cells.shape[dim] - width, cells.shape[dim], axis=dim)
        cells = jnp.concatenate(
            [
                lax.ppermute(tail, axis, [(i, (i + 1) % count) for i in range(ends)]),
                cells,
                lax.ppermute(head, axis, [((i + 1) % count, i) for i in range(ends)]),
            ],
            axis=dim,
        )
    return cells


def local(
    feature_maps, query_frame, query_row, query_col, ema_decay, dw_kernel, pw_weight, out_weight
):
    frames_here, rows_here, map_width, channels = feature_maps.shape
    num_queries = query_frame.shape[0]
    first_frame = lax.axis_index("tm") * frames_here
    first_row = lax.axis_index("space") * rows_here
    map_height = rows_here * lax.axis_size("space")
    local_frame = query_frame - first_frame
    local_row = query_row - first_row
    owned = (
        (local_frame >= 0)
        & (local_frame < frames_here)
        & (local_row >= 0)
        & (local_row < rows_here)
    )
    picked = feature_maps[
        jnp.clip(local_frame, 0, frames_here - 1), jnp.clip(local_row, 0, rows_here - 1), query_col
    ]
    contrib = jnp.where(owned[:, None], picked.astype(jnp.float32), 0.0)
    query_feats = lax.psum(contrib, ("tm", "space")).astype(jnp.bfloat16)
    scale = 1.0 / math.sqrt(channels)
    col_coord = jnp.arange(map_width, dtype=jnp.int32).astype(jnp.float32) / map_width
    row_coord = (first_row + jnp.arange(rows_here, dtype=jnp.int32)).astype(
        jnp.float32
    ) / map_height
    highest_list, total_list, pos_list, feat_list = ([], [], [], [])
    frame_index = 0
    frame_map = feature_maps[frame_index].reshape(rows_here * map_width, channels)
    scores = (
        lax.dot_general(
            query_feats, frame_map, (((1,), (1,)), ((), ())), preferred_element_type=jnp.float32
        )
        * scale
    )
    highest = jnp.max(scores, axis=1)
    weights_exp = jnp.exp(scores - highest[:, None])
    highest_list.append(highest)
    total_list.append(jnp.sum(weights_exp, axis=1))
    grid = weights_exp.reshape(num_queries, rows_here, map_width)
    col_part = jnp.sum(jnp.sum(grid, axis=1) * col_coord[None, :], axis=1)
    line_portion = jnp.sum(jnp.sum(grid, axis=2) * row_coord[None, :], axis=1)
    pos_list.append(jnp.stack([col_part, line_portion], 1))
    feat_list.append(
        jnp.dot(weights_exp.astype(jnp.bfloat16), frame_map, preferred_element_type=jnp.float32)
    )
    highest = jnp.stack(highest_list)
    totals = jnp.stack(total_list)
    pos_sum = jnp.stack(pos_list)
    feat_sum = jnp.stack(feat_list)
    top_value = lax.pmax(highest, "space")
    factor = jnp.exp(highest - top_value)
    grand_total, pos_all, feat_all = lax.psum(
        (factor * totals, factor[..., None] * pos_sum, factor[..., None] * feat_sum), "space"
    )
    position = pos_all / grand_total[..., None]
    focused_result = (feat_all / grand_total[..., None]).astype(jnp.bfloat16)
    padded = with_halo(focused_result, (("tm", 0),), 1).astype(jnp.float32)
    depth = jnp.zeros((frames_here, num_queries, channels), jnp.float32)
    for tap in range(dw_kernel.shape[0]):
        depth = depth + dw_kernel[tap][None, None, :] * padded[tap : tap + frames_here]
    hidden = jax.nn.gelu(depth).astype(jnp.bfloat16)
    mixed = jnp.dot(
        hidden.reshape(-1, channels), pw_weight, preferred_element_type=jnp.float32
    ).reshape(frames_here, num_queries, channels)
    refined = focused_result.astype(jnp.float32) + mixed
    carried = jnp.zeros((num_queries, channels), jnp.float32)
    retain_prod = jnp.ones((channels,), jnp.float32)
    local_states, local_prods = ([], [])
    frame_index = 0
    retain = ema_decay[frame_index]
    carried = retain[None, :] * carried + (1.0 - retain[None, :]) * refined[frame_index]
    retain_prod = retain_prod * retain
    local_states.append(carried)
    local_prods.append(retain_prod)
    all_prods, all_ends = (
        lax.all_gather(retain_prod[None], "tm", axis=0, tiled=True),
        lax.all_gather(carried[None], "tm", axis=0, tiled=True),
    )
    position_tm = lax.axis_index("tm")

    def fold_step(source, running):
        advanced = all_prods[source][None, :] * running + all_ends[source]
        return jnp.where(source < position_tm, advanced, running)

    incoming = lax.fori_loop(
        0, lax.axis_size("tm"), fold_step, jnp.zeros((num_queries, channels), jnp.float32)
    )
    memory = jnp.stack(local_states) + jnp.stack(local_prods)[:, None, :] * incoming[None]
    delta = jnp.einsum("tqc,kc->tkq", memory, out_weight, precision=lax.Precision.HIGHEST)
    return jnp.transpose(position, (0, 2, 1)) + delta


def solution(mesh):
    placed = (
        P(("video", "tm"), "space", None, None),
        P("video"),
        P("video"),
        P("video"),
        P(("video", "tm"), None),
        P(),
        P(),
        P(),
    )
    return jax.shard_map(
        local, mesh=mesh, in_specs=placed, out_specs=P(("video", "tm"), None, None), check_vma=False
    )
```

profile of v0, /device:TPU:1, one launch (start us, length us, event | category | flops | bytes accessed | tf_op | source)
XLA Modules:
  0.0 416.0 jit_solution(9454271297745757524)
XLA Ops:
  6.5 0.0 copy-start
  6.5 0.8 compare_and_fusion
  7.4 0.7 fusion.41
  8.1 3.1 gather_fusion
  11.3 0.1 convert_select_fusion
  11.4 250.4 %all-reduce.5 = bf16[512,128]{1,0:T(8,128)(2,1)S(1)} all-reduce(f32[512,128]{1,0:T(8,128)S(1)} %convert_select_fusion), channel_id=1, replica_groups=mesh['video'=4,'tm'=16,'space'=4] {'tm','space'}, use_global_device_ids=true, to_apply=%region_0.1 | all-reduce | flops 65536 | bytes 393216 | tf_op jit(solution)/shard_map/psum | solution.py:46
  261.8 2.3 multiply_reduce_fusion
  264.1 7.0 %fusion.50 = (f32[512]{0:T(512)S(1)}, f32[512,7680]{1,0:T(8,128)}) fusion(f32[512]{0:T(512)S(1)} %get-tuple-element.139, f32[512,7680]{1,0:T(8,128)S(1)} %get-tuple-element.140), kind=kLoop, calls=%fused_computation.74 | loop fusion | flops 11795968 | bytes 31461376 | tf_op jit(solution)/shard_map/reduce_sum | solution.py:64
  271.1 6.0 %pmax.7 = f32[1,512]{1,0:T(1,128)S(1)} all-reduce(f32[1,512]{1,0:T(1,128)S(1)} %bitcast.66), channel_id=1, replica_groups=mesh['video'=4,'tm'=16,'space'=4] {'space'}, use_global_device_ids=true, to_apply=%region_2.3 | all-reduce | flops 512 | bytes 4096 | tf_op jit(solution)/shard_map/pmax | solution.py:76
  277.1 8.4 %fusion.7 = f32[1,512,128]{2,1,0:T(8,128)} fusion(bf16[7680,128]{1,0:T(8,128)(2,1)S(1)} %bitcast.62, f32[512,7680]{1,0:T(8,128)} %get-tuple-element.135, f32[512]{0:T(512)S(1)} %bitcast.64), kind=kOutput, calls=%fused_computation.11 | convolution fusion | flops 1010630656 | bytes 17958912 | tf_op jit(solution)/shard_map/dot_general | solution.py:70
  285.5 0.0 all-reduce.4.cloned.1.call-update
  285.5 0.0 all-gather.3.cloned.1.call-start
  285.5 15.7 %copy.10 = f32[512,7680]{0,1:T(8,128)} copy(f32[512,7680]{1,0:T(8,128)} %get-tuple-element.135) | data formatting | bytes 31457280 | tf_op jit(solution)/shard_map/exp | solution.py:62
  301.3 7.9 %fusion.48 = (f32[512,240]{0,1:T(8,128)S(1)}, f32[512,32]{0,1:T(8,128)S(1)}) fusion(f32[512,32,240]{0,2,1:T(8,128)} %bitcast.63), kind=kLoop, calls=%fused_computation.72 | loop fusion | flops 7725056 | bytes 16285696 | tf_op jit(solution)/shard_map/reduce_sum | solution.py:66
  309.2 0.1 multiply_reduce_fusion.2
  309.3 0.1 multiply_reduce_fusion.1
  309.4 7.5 %all-reduce = (f32[512]{0:T(512)S(1)}, f32[1,512,2]{1,2,0:T(2,128)S(1)}) all-reduce(f32[512]{0:T(512)S(1)} %bitcast.70, f32[1,512,2]{1,2,0:T(2,128)S(1)} %maximum_multiply_fusion), channel_id=1, replica_groups=mesh['video'=4,'tm'=16,'space'=4] {'space'}, use_global_device_ids=true, to_apply=%region_9.10 | all-reduce | flops 1536 | bytes 12288 | tf_op jit(solution)/shard_map/psum | solution.py:78
  317.0 15.6 %all-reduce.4.cloned.1.call-done = f32[1,512,128]{2,1,0:T(8,128)} async-done(((f32[1,512,128]{2,1,0:T(8,128)}), f32[1,512,128]{2,1,0:T(8,128)}) %all-reduce.4.cloned.1.call-update) | async-done | bytes 262160 | tf_op jit(solution)/shard_map/psum | solution.py:78
  332.6 1.1 divide_convert_fusion
  333.7 4.7 %collective-permute-start.1 = (bf16[1,512,128]{2,1,0:T(8,128)(2,1)S(1)}, bf16[1,512,128]{2,1,0:T(8,128)(2,1)S(1)}, u32[]{:S(2)}, u32[]{:S(2)}) collective-permute-start(bf16[1,512,128]{2,1,0:T(8,128)(2,1)S(1)} %divide_convert_fusion), channel_id=1, source_target_pairs={{4,0},{8,4},{12,8},{16,12},{20,16},{24,20},{28,24},{32,28},{36,32}... | collective-permute-start | bytes 393224 | tf_op jit(solution)/shard_map/ppermute | solution.py:19
  338.4 3.1 collective-permute-start
  341.5 0.7 collective-permute-done.1
  342.2 1.2 collective-permute-done
  343.4 0.1 maximum_convert_fusion
  343.5 0.0 copy-done.4
  343.5 0.9 multiply_add_fusion
  344.4 0.0 all-gather.3.cloned.1.call-update
  344.5 18.6 %all-gather = f32[16,1,128]{2,1,0:T(1,128)S(1)} all-gather(f32[1,1,128]{2,1,0:T(1,128)S(1)} %bitcast.73), channel_id=1, replica_groups=mesh['video'=4,'tm'=16,'space'=4] {'tm'}, dimensions={0}, use_global_device_ids=true | all-gather | bytes 8704 | tf_op jit(solution)/shard_map/all_gather | solution.py:102
  363.0 26.2 %all-gather.3.cloned.1.call-done = f32[16,512,128]{2,1,0:T(8,128)} async-done(((f32[1,512,128]{2,1,0:T(8,128)}), f32[16,512,128]{2,1,0:T(8,128)}) %all-gather.3.cloned.1.call-update) | async-done | bytes 4194320 | tf_op jit(solution)/shard_map/all_gather | solution.py:103
  389.2 19.0 %while.14 = (s32[]{:T(128)}, f32[512,128]{1,0:T(8,128)S(1)}, s32[]{:T(128)}, f32[16,128]{1,0:T(8,128)S(1)}, f32[16,512,128]{2,1,0:T(8,128)}, /*index=5*/s32[]{:T(128)}, s32[]{:T(128)}) while((s32[]{:T(128)}, f32[512,128]{1,0:T(8,128)S(1)}, s32[]{:T(128)}, f32[16,128]{1,0:T(8,128)S(1)}, f32[16,512,128]{2,1,0:T(8,128)}, ...), condition=%wide.region_12.13_spmd.clone, body=%wide.region_11.12_spmd.clone.sunk | while | flops 262148 | bytes 788081 | solution.py:111
  389.2 1.1 fusion.57
  390.4 1.1 fusion.57
  391.6 1.1 fusion.57
  392.8 1.1 fusion.57
  394.0 1.1 fusion.57
  395.1 1.1 fusion.57
  396.3 1.1 fusion.57
  397.5 1.1 fusion.57
  398.7 1.1 fusion.57
  399.9 1.1 fusion.57
  401.1 1.1 fusion.57
  402.3 1.1 fusion.57
  403.5 1.1 fusion.57
  404.7 1.1 fusion.57
  405.9 1.1 fusion.57
  407.0 1.1 fusion.57
  408.2 0.0 copy-done.3
  408.2 1.0 fusion.10
  (32 shorter events, 0.2 us)
Async XLA Ops:
  6.5 1.6 copy-start
  6.5 326.1 %all-reduce.4.cloned.1.call-start = ((), (), s32[]{:S(2)}) async-start(), calls=%async_computation | async-start | bytes 524288 | tf_op jit(solution)/shard_map/psum | solution.py:78
  285.5 103.7 %all-gather.3.cloned.1.call-start = ((), (), s32[]{:S(2)}) async-start(), calls=%async_computation.1 | async-start | bytes 4456448 | tf_op jit(solution)/shard_map/all_gather | solution.py:103
  301.3 8.1 %copy-start.1 = (f32[1,128]{1,0:T(1,128)S(1)}, f32[1,128]{1,0:T(1,128)}, u32[]{:S(2)}) copy-start(f32[1,128]{1,0:T(1,128)} %param.14) | copy-start | bytes 1540
  301.3 15.7 %copy-start.2 = (f32[3,128]{1,0:T(4,128)S(1)}, f32[3,128]{1,0:T(4,128)}, u32[]{:S(2)}) copy-start(f32[3,128]{1,0:T(4,128)} %param.15) | copy-start | bytes 4612
  301.3 42.2 %copy-start.4 = (bf16[128,128]{1,0:T(8,128)(2,1)S(1)}, bf16[128,128]{1,0:T(8,128)(2,1)}, u32[]{:S(2)}) copy-start(bf16[128,128]{1,0:T(8,128)(2,1)} %param.16) | copy-start | bytes 98308
  301.3 106.9 %copy-start.3 = (f32[2,128]{1,0:T(2,128)S(1)}, f32[2,128]{1,0:T(2,128)}, u32[]{:S(2)}) copy-start(f32[2,128]{1,0:T(2,128)} %param.17) | copy-start | bytes 3076
  333.7 8.5 %collective-permute-start.1 = (bf16[1,512,128]{2,1,0:T(8,128)(2,1)S(1)}, bf16[1,512,128]{2,1,0:T(8,128)(2,1)S(1)}, u32[]{:S(2)}, u32[]{:S(2)}) collective-permute-start(bf16[1,512,128]{2,1,0:T(8,128)(2,1)S(1)} %divide_convert_fusion), channel_id=1, source_target_pairs={{4,0},{8,4},{12,8},{16,12},{20,16},{24,20},{28,24},{32,28},{36,32}... | collective-permute-start | bytes 393224 | tf_op jit(solution)/shard_map/ppermute | solution.py:19
  338.4 5.0 %collective-permute-start = (bf16[1,512,128]{2,1,0:T(8,128)(2,1)S(1)}, bf16[1,512,128]{2,1,0:T(8,128)(2,1)S(1)}, u32[]{:S(2)}, u32[]{:S(2)}) collective-permute-start(bf16[1,512,128]{2,1,0:T(8,128)(2,1)S(1)} %divide_convert_fusion), channel_id=1, source_target_pairs={{0,4},{4,8},{8,12},{12,16},{16,20},{20,24},{24,28},{28,32},{32,36}... | collective-permute-start | bytes 393224 | tf_op jit(solution)/shard_map/ppermute | solution.py:17
Sparse Core Ops, SparseCore 0:
  285.6 46.9 all-reduce.3
  344.6 44.5 all-gather.2
where the time goes:
time: 417 us; the launch traced here: 416 us
  blocking collectives  282 us (68%)
  waiting for transfers between devices  43.7 us (10%)
  other arithmetic  36.3 us (9%)
  local copies, waits for them, and re-layouts  19 us (5%)
  between operations  13.6 us (3%)
  matrix products  12.6 us (3%)
  starting transfers between devices  7.84 us (2%)
    psum x1, blocking collectives, local(): query_feats = lax.psum(contrib, ('tm', 'space')).astype(jnp.bfloat16)  250 us
    all_gather x1, waiting for transfers between devices, local(): lax.all_gather(carried[None], 'tm', axis=0, tiled=True)  26.2 us
    all_gather x1, blocking collectives, local(): lax.all_gather(retain_prod[None], 'tm', axis=0, tiled=True)  18.6 us
    select_n x16, other arithmetic, fold_step(): return jnp.where(source < position_tm, advanced, running)  18.4 us
    exp x1, local copies, waits for them, and re-layouts, local(): weights_exp = jnp.exp(scores - highest[:, None])  15.7 us
    psum x1, waiting for transfers between devices, local(): lax.psum((factor * totals, factor[..., None] * pos_sum, factor[..., None]...  15.6 us
    dot_general x1, matrix products, local(): jnp.dot(weights_exp.astype(jnp.bfloat16), frame_map, preferred_element_ty...  8.38 us
  transfers between devices with their start and end apart: 4, of which 4 were waited for; matrix products, arithmetic and copies ran while one was open for 6% of the time, Pallas kernels for 0%

commit v1 on v0

v1 whole, which is shorter than its diff:
```python
import functools
import math

import jax
import jax.numpy as jnp
from jax import lax
from jax.experimental import pallas as pl
from jax.experimental.pallas import tpu as pltpu
from jax.sharding import PartitionSpec as P

MESH = pl.DeviceIdType.MESH
F32 = jnp.float32
BF16 = jnp.bfloat16


def kernel(
    dims, fm, q_frame, q_row, q_col, decay, taps, pw, out_w, out,
    keys, keys32, keys_t, contrib32, contrib, rs_in, q_own, q_all, q_t, decay_all, tap_cols,
    pw_t, proj, scores, acc, part, part_in, att_own, att_in, term, term_in,
    key_sem, rs_send, rs_recv, ag_send, ag_recv, dec_send, dec_recv,
    part_send, part_recv, halo_send, halo_recv, term_send, term_recv,
):
    n_tm, n_sp, n_q, rows, width, ch, height = dims
    group = n_tm * n_sp
    per_home = n_q // group
    q_blk = n_q // n_sp
    n_pos = rows * width
    t = lax.axis_index("tm")
    y = lax.axis_index("space")
    me = y * n_tm + t

    def peer(r):
        other = lax.rem(me + r, group)
        return {"tm": lax.rem(other, n_tm), "space": lax.div(other, n_tm)}

    barrier = pltpu.get_barrier_semaphore()

    @pl.loop(1, group)
    def _(r):
        pl.semaphore_signal(barrier, inc=1, device_id=peer(r), device_id_type=MESH)

    load = pltpu.make_async_copy(fm, keys, key_sem)
    load.start()
    load.wait()

    step = 256

    @pl.loop(0, n_pos // step)
    def _(j):
        at = pl.multiple_of(j * step, step)
        keys32[pl.ds(at, step), :] = keys[pl.ds(at, step), :].astype(F32)

    keys32[pl.ds(n_pos, 8), :] = jnp.zeros((8, ch), F32)
    first_row = y * rows

    @pl.loop(0, n_q // 8)
    def _(i):
        for u in range(8):
            q = i * 8 + u
            row = q_row[q] - first_row
            mine = (q_frame[q] == t) & (row >= 0) & (row < rows)
            at = jnp.where(mine, row * width + q_col[q], n_pos)
            contrib32[pl.ds(q, 1), :] = keys32[pl.ds(at, 1), :]

    contrib[...] = contrib32[...].reshape(group, per_home, ch).astype(BF16)

    pl.semaphore_wait(barrier, group - 1)

    def rs_copy(r):
        other = lax.rem(me + r, group)
        return pltpu.make_async_remote_copy(
            contrib.at[other], rs_in.at[r - 1], rs_send, rs_recv,
            device_id=peer(r), device_id_type=MESH,
        )

    @pl.loop(1, group)
    def _(r):
        rs_copy(r).start()

    decay_all[t] = decay[...]

    @pl.loop(1, n_tm)
    def _(r):
        pltpu.make_async_remote_copy(
            decay, decay_all.at[t], dec_send, dec_recv,
            device_id={"tm": lax.rem(t + r, n_tm)}, device_id_type=MESH,
        ).start()

    @pl.loop(0, n_pos // 128)
    def _(j):
        at = pl.multiple_of(j * 128, 128)
        keys_t[pl.ds(0, ch), pl.ds(at, 128)] = keys32[pl.ds(at, 128), :].T.astype(BF16)

    place = lax.broadcasted_iota(jnp.int32, (16, n_pos), 1).astype(F32)
    line = jnp.floor((place + 0.5) * (1.0 / width))
    col = place - line * width
    line = line + (y * rows).astype(F32)
    kind = lax.broadcasted_iota(jnp.int32, (16, n_pos), 0)
    extra = jnp.where(kind == 0, 1.0, jnp.where(kind == 1, col, jnp.where(kind == 2, line, 0.0)))
    keys_t[pl.ds(ch, 16), :] = extra.astype(BF16)

    all_rs = pltpu.make_async_remote_copy(
        contrib.at[pl.ds(0, group - 1)], rs_in, rs_send, rs_recv,
        device_id=peer(1), device_id_type=MESH,
    )
    all_rs.wait_recv()
    total = contrib[me].astype(F32) + jnp.sum(rs_in[...].astype(F32), axis=0)
    q_own[...] = total.astype(BF16)
    q_all[me] = total.astype(BF16)

    @pl.loop(1, group)
    def _(r):
        pltpu.make_async_remote_copy(
            q_own, q_all.at[me], ag_send, ag_recv, device_id=peer(r), device_id_type=MESH
        ).start()

    eye = lax.broadcasted_iota(jnp.int32, (ch, ch), 0) == lax.broadcasted_iota(
        jnp.int32, (ch, ch), 1
    )
    for k in range(3):
        column = jnp.sum(jnp.where(eye, taps[pl.ds(k, 1), :], 0.0), axis=1, keepdims=True)
        tap_cols[k] = jnp.broadcast_to(column, (ch, q_blk))
    pw_t[...] = pw[...].astype(F32).T.astype(BF16)
    all_dec = pltpu.make_async_remote_copy(
        decay_all.at[pl.ds(0, n_tm - 1)], decay_all.at[pl.ds(0, n_tm - 1)], dec_send, dec_recv,
        device_id={"tm": lax.rem(t + 1, n_tm)}, device_id_type=MESH,
    )
    all_dec.wait()
    run = out_w[...] * (1.0 - decay[...])
    gain = jnp.zeros_like(run)
    for frame in range(n_tm):
        kept = gain if frame == 0 else gain * decay_all[frame]
        gain = jnp.where(t == frame, run, jnp.where(t < frame, kept, 0.0))
        proj[frame] = gain

    all_ag = pltpu.make_async_remote_copy(
        rs_in, rs_in, ag_send, ag_recv, device_id=peer(1), device_id_type=MESH
    )
    all_ag.wait_recv()
    q_t[...] = q_all[...].astype(F32).reshape(n_q, ch).T.astype(BF16)

    half = n_q // 2
    pair = lax.div(y, 2)
    scale = math.log2(math.e) / math.sqrt(ch)
    t1 = 768
    t2 = 1536

    def part_copy(slot, to):
        return pltpu.make_async_remote_copy(
            part.at[slot], part_in.at[slot - 1], part_send.at[slot - 1], part_recv.at[slot - 1],
            device_id={"space": to}, device_id_type=MESH,
        )

    for chunk in range(2):
        which = (1 - pair) if chunk == 0 else pair
        q_at = pl.multiple_of(which * half, half)

        def first(j, top):
            at = pl.multiple_of(j * t1, t1)
            s = jnp.dot(
                keys[pl.ds(at, t1), :], q_t[:, pl.ds(q_at, half)], preferred_element_type=F32
            )
            scores[pl.ds(at, t1), :] = s
            return jnp.maximum(top, jnp.max(s.reshape(t1 // 8, 8, half), axis=0))

        top = lax.fori_loop(0, n_pos // t1, first, jnp.full((8, half), -jnp.inf, F32))
        top = jnp.max(top, axis=0, keepdims=True)
        acc[...] = jnp.zeros_like(acc)

        @pl.loop(0, n_pos // t2)
        def _(j):
            at = pl.multiple_of(j * t2, t2)
            e = jnp.exp2((scores[pl.ds(at, t2), :] - top) * scale).astype(BF16)
            acc[...] += jnp.dot(keys_t[:, pl.ds(at, t2)], e, preferred_element_type=F32)

        for side in range(2):
            to = which * 2 + side
            slot = lax.rem(to - y + n_sp, n_sp)
            lanes = slice(side * q_blk, (side + 1) * q_blk)
            part[slot, pl.ds(0, ch + 8), :] = acc[pl.ds(0, ch + 8), lanes]
            part[slot, pl.ds(ch + 8, 8), :] = jnp.broadcast_to(top[:, lanes], (8, q_blk))
            if chunk == 0:
                part_copy(slot, to).start()
            else:

                @pl.when(slot != 0)
                def _():
                    part_copy(slot, to).start()

    for slot in range(1, n_sp):
        part_copy(slot, y).wait_recv()
    own = part[0]
    parts = [own] + [part_in[i] for i in range(n_sp - 1)]
    tops = [p[ch + 8 : ch + 9] for p in parts]
    best = functools.reduce(jnp.maximum, tops)
    mixed = None
    for p, m in zip(parts, tops):
        v = p[: ch + 8] * jnp.exp2((m - best) * scale)
        mixed = v if mixed is None else mixed + v
    inverse = 1.0 / mixed[ch : ch + 1]
    position = mixed[ch + 1 : ch + 3] * inverse
    unit = jnp.where(
        lax.broadcasted_iota(jnp.int32, (2, q_blk), 0) == 0, 1.0 / width, 1.0 / height
    )
    position = position * unit
    att = (mixed[:ch] * inverse).astype(BF16)
    att_own[...] = att

    def halo(side):
        to = lax.rem(t + (1 if side == 0 else n_tm - 1), n_tm)
        return pltpu.make_async_remote_copy(
            att_own, att_in.at[side], halo_send.at[side], halo_recv.at[side],
            device_id={"tm": to}, device_id_type=MESH,
        )

    halo(0).start()
    halo(1).start()
    att = att.astype(F32)
    mid = att * tap_cols[1]
    halo(0).wait_recv()
    halo(1).wait_recv()
    before = jnp.where(t > 0, att_in[0].astype(F32), 0.0)
    after = jnp.where(t < n_tm - 1, att_in[1].astype(F32), 0.0)
    depth = tap_cols[0] * before + mid + tap_cols[2] * after
    hidden = jax.nn.gelu(depth).astype(BF16)
    refined = att + jnp.dot(pw_t[...], hidden, preferred_element_type=F32)
    terms = jnp.dot(
        proj[...].reshape(2 * n_tm, ch), refined, preferred_element_type=F32,
        precision=lax.Precision.HIGHEST,
    )
    term[...] = terms.reshape(n_tm, 2, q_blk)
    term[t] = term[t] + position
    term_in[me] = term[t]

    @pl.loop(1, group)
    def _(r):
        other = peer(r)
        pltpu.make_async_remote_copy(
            term.at[other["tm"]], term_in.at[me], term_send, term_recv,
            device_id=other, device_id_type=MESH,
        ).start()

    all_term = pltpu.make_async_remote_copy(
        term_in.at[pl.ds(0, group - 1)], term_in.at[pl.ds(0, group - 1)], term_send, term_recv,
        device_id=peer(1), device_id_type=MESH,
    )
    all_term.wait()
    for b in range(n_sp):
        out[:, b * q_blk : (b + 1) * q_blk] = jnp.sum(term_in[pl.ds(b * n_tm, n_tm)], axis=0)

    all_rs.wait_send()
    all_ag.wait_send()
    for slot in range(1, n_sp):
        part_copy(slot, y).wait_send()
    halo(0).wait_send()
    halo(1).wait_send()


def solution(mesh):
    n_tm, n_sp = mesh.shape["tm"], mesh.shape["space"]

    def local(fm, q_frame, q_row, q_col, decay, taps, pw, out_w):
        frames, rows, width, ch = fm.shape
        n_q = q_frame.shape[0]
        n_pos = rows * width
        group = n_tm * n_sp
        per_home = n_q // group
        q_blk = n_q // n_sp
        half = n_q // 2
        dims = (n_tm, n_sp, n_q, rows, width, ch, rows * n_sp)
        smem = pl.BlockSpec(memory_space=pltpu.SMEM)
        vmem = pl.BlockSpec(memory_space=pltpu.VMEM)
        dma = pltpu.SemaphoreType.DMA
        out = pl.pallas_call(
            functools.partial(kernel, dims),
            out_shape=jax.ShapeDtypeStruct((2, n_q), F32),
            in_specs=[pl.BlockSpec(memory_space=pl.ANY), smem, smem, smem, vmem, vmem, vmem, vmem],
            out_specs=vmem,
            scratch_shapes=[
                pltpu.VMEM((n_pos, ch), BF16),
                pltpu.VMEM((n_pos + 8, ch), F32),
                pltpu.VMEM((ch + 16, n_pos), BF16),
                pltpu.VMEM((n_q, ch), F32),
                pltpu.VMEM((group, per_home, ch), BF16),
                pltpu.VMEM((group - 1, per_home, ch), BF16),
                pltpu.VMEM((per_home, ch), BF16),
                pltpu.VMEM((group, per_home, ch), BF16),
                pltpu.VMEM((ch, n_q), BF16),
                pltpu.VMEM((n_tm, 1, ch), F32),
                pltpu.VMEM((3, ch, q_blk), F32),
                pltpu.VMEM((ch, ch), BF16),
                pltpu.VMEM((n_tm, 2, ch), F32),
                pltpu.VMEM((n_pos, half), F32),
                pltpu.VMEM((ch + 16, half), F32),
                pltpu.VMEM((n_sp, ch + 16, q_blk), F32),
                pltpu.VMEM((n_sp - 1, ch + 16, q_blk), F32),
                pltpu.VMEM((ch, q_blk), BF16),
                pltpu.VMEM((2, ch, q_blk), BF16),
                pltpu.VMEM((n_tm, 2, q_blk), F32),
                pltpu.VMEM((group, 2, q_blk), F32),
                dma, dma, dma, dma, dma, dma, dma,
                dma((n_sp - 1,)), dma((n_sp - 1,)), dma((2,)), dma((2,)), dma, dma,
            ],
            compiler_params=pltpu.CompilerParams(collective_id=0, has_side_effects=True),
        )(fm.reshape(n_pos, ch), q_frame, q_row, q_col, decay, taps, pw, out_w)
        return out[None]

    placed = (
        P(("video", "tm"), "space", None, None),
        P("video"),
        P("video"),
        P("video"),
        P(("video", "tm"), None),
        P(),
        P(),
        P(),
    )
    return jax.shard_map(
        local, mesh=mesh, in_specs=placed, out_specs=P(("video", "tm"), None, None), check_vma=False
    )
```

time: 417 us -> 51.7 us (0.12)
  blocking collectives: 282 us -> 0 us
  Pallas kernels: 0 us -> 50.2 us
  waiting for transfers between devices: 43.7 us -> 0 us
  other arithmetic: 36.3 us -> 0 us
  local copies, waits for them, and re-layouts: 19 us -> 1.28 us
  between operations: 13.6 us -> 0.01 us
  matrix products: 12.6 us -> 0 us
  starting transfers between devices: 7.84 us -> 0 us
    psum x2 -> x0, blocking collectives: 258 us -> none  [the longest x1 250 us: local(): query_feats = lax.psum(contrib, ('tm', 'space')).astype(jnp.bfloat16)]
    pallas_call x0 -> x1, Pallas kernels: none -> 50.2 us  [local(): pl.pallas_call(functools.partial(kernel, dims), out_shape=jax.ShapeDtypeS...]
    all_gather x1 -> x0, waiting for transfers between devices: 26.2 us -> none  [local(): lax.all_gather(carried[None], 'tm', axis=0, tiled=True)]
    all_gather x1 -> x0, blocking collectives: 18.6 us -> none  [local(): lax.all_gather(retain_prod[None], 'tm', axis=0, tiled=True)]
    select_n x17 -> x0, other arithmetic: 18.5 us -> none  [the longest x16 18.4 us: fold_step(): return jnp.where(source < position_tm, advanced, running)]
    exp x1 -> x0, local copies, waits for them, and re-layouts: 15.7 us -> none  [local(): weights_exp = jnp.exp(scores - highest[:, None])]
    psum x1 -> x0, waiting for transfers between devices: 15.6 us -> none  [local(): lax.psum((factor * totals, factor[..., None] * pos_sum, factor[..., None]...]
    reduce_sum x4 -> x0, other arithmetic: 15.1 us -> none  [the longest x2 8 us: local(): col_part = jnp.sum(jnp.sum(grid, axis=1) * col_coord[None, :], axis=1)]
  transfers between devices with their start and end apart: 4 -> 0, of which waited for: 4 -> 0; matrix products, arithmetic and copies ran while one was open for 6% -> 0% of each run, Pallas kernels for 0% -> 0%
where the time goes in v1:
time: 51.7 us; the launch traced here: 51.5 us
  Pallas kernels  50.2 us (97%)
  local copies, waits for them, and re-layouts  1.28 us (2%)
    pallas_call x1, Pallas kernels, local(): pl.pallas_call(functools.partial(kernel, dims), out_shape=jax.ShapeDtypeS...  50.2 us
    unnamed x1, local copies, waits for them, and re-layouts  1.28 us

profile of v1, /device:TPU:1, one launch (start us, length us, event | category | flops | bytes accessed | tf_op | source)
XLA Modules:
  0.0 51.5 jit_solution(4553383838387268459)
XLA Ops:
  0.0 50.2 %shard_map.82 = f32[2,512]{1,0:T(2,128)} custom-call(bf16[7680,128]{1,0:T(8,128)(2,1)} %bitcast.2, s32[512]{0:T(512)} %q_frame.1, s32[512]{0:T(512)} %q_row.1, s32[512]{0:T(512)} %q_col.1, f32[1,128]{1,0:T(1,128)} %decay.1, f32[3,128]{1,0:T(4,128)} %taps.1, bf16[128,128]{1,0:T(8,128)(2,1)} %pw.1, f32[2,128]{1,0:T(2,128)} %out_w.1), custom_call_target="tpu_custom_call" | custom-call | tf_op jit(solution)/shard_map/pallas_call | solution.py:274
  50.2 1.3 %copy.10 = f32[1,2,512]{2,1,0:T(2,128)} copy(f32[1,2,512]{2,1,0:T(2,128)} %bitcast.3) | data formatting | bytes 8192

commit v2 on v1

--- a/solution.py
+++ b/solution.py
@@ -15,32 +15,42 @@
 
 def kernel(
     dims, fm, q_frame, q_row, q_col, decay, taps, pw, out_w, out,
-    keys, keys32, keys_t, contrib32, contrib, rs_in, q_own, q_all, q_t, decay_all, tap_cols,
-    pw_t, proj, scores, acc, part, part_in, att_own, att_in, term, term_in,
-    key_sem, rs_send, rs_recv, ag_send, ag_recv, dec_send, dec_recv,
-    part_send, part_recv, halo_send, halo_recv, term_send, term_recv,
+    keys, keys32, keys_t, contrib32, contrib, rs_in, z_own, z_in, q_own, q_all, q_t, decay_all,
+    tap_cols, pw_t, proj, even, odd, acc, part, part_in, att_own, att_in, term, term_in, row_own,
+    row_all, key_sem, rs_send, rs_recv, z_send, z_recv, ag_send, ag_recv, dec_send, dec_recv,
+    part_send, part_recv, halo_send, halo_recv, term_send, term_recv, row_send, row_recv,
 ):
     n_tm, n_sp, n_q, rows, width, ch, height = dims
-    group = n_tm * n_sp
-    per_home = n_q // group
+    n_z = n_tm // 2
+    plane = 2 * n_sp
     q_blk = n_q // n_sp
     n_pos = rows * width
     t = lax.axis_index("tm")
     y = lax.axis_index("space")
-    me = y * n_tm + t
-
-    def peer(r):
-        other = lax.rem(me + r, group)
-        return {"tm": lax.rem(other, n_tm), "space": lax.div(other, n_tm)}
-
-    barrier = pltpu.get_barrier_semaphore()
-
-    @pl.loop(1, group)
-    def _(r):
-        pl.semaphore_signal(barrier, inc=1, device_id=peer(r), device_id_type=MESH)
+    z = lax.div(t, 2)
+    core = lax.rem(t, 2)
+    me = y * 2 + core
+
+    def in_plane(r):
+        other = lax.rem(me + r, plane)
+        return other, {"tm": z * 2 + lax.rem(other, 2), "space": lax.div(other, 2)}
+
+    def along_z(r):
+        return {"tm": lax.rem(t + 2 * r, n_tm)}
 
     load = pltpu.make_async_copy(fm, keys, key_sem)
     load.start()
+    barrier = pltpu.get_barrier_semaphore()
+    for r in range(1, n_tm):
+        pl.semaphore_signal(
+            barrier, inc=1, device_id={"tm": lax.rem(t + r, n_tm)}, device_id_type=MESH
+        )
+    for r in range(1, n_sp):
+        for c in range(2):
+            pl.semaphore_signal(
+                barrier, inc=1, device_id={"tm": z * 2 + c, "space": lax.rem(y + r, n_sp)},
+                device_id_type=MESH,
+            )
     load.wait()
 
     step = 256
@@ -62,19 +72,18 @@
             at = jnp.where(mine, row * width + q_col[q], n_pos)
             contrib32[pl.ds(q, 1), :] = keys32[pl.ds(at, 1), :]
 
-    contrib[...] = contrib32[...].reshape(group, per_home, ch).astype(BF16)
-
-    pl.semaphore_wait(barrier, group - 1)
+    contrib[...] = contrib32[...].reshape(plane, n_q // plane, ch).astype(BF16)
+
+    pl.semaphore_wait(barrier, n_tm - 1 + plane - 2)
 
     def rs_copy(r):
-        other = lax.rem(me + r, group)
+        other, device = in_plane(r)
         return pltpu.make_async_remote_copy(
             contrib.at[other], rs_in.at[r - 1], rs_send, rs_recv,
-            device_id=peer(r), device_id_type=MESH,
-        )
-
-    @pl.loop(1, group)
-    def _(r):
+            device_id=device, device_id_type=MESH,
+        )
+
+    for r in range(1, plane):
         rs_copy(r).start()
 
     decay_all[t] = decay[...]
@@ -84,6 +93,17 @@
         pltpu.make_async_remote_copy(
             decay, decay_all.at[t], dec_send, dec_recv,
             device_id={"tm": lax.rem(t + r, n_tm)}, device_id_type=MESH,
+        ).start()
+
+    all_rs = pltpu.make_async_remote_copy(
+        rs_in, rs_in, rs_send, rs_recv, device_id=in_plane(1)[1], device_id_type=MESH
+    )
+    all_rs.wait_recv()
+    total = contrib[me].astype(F32) + jnp.sum(rs_in[...].astype(F32), axis=0)
+    z_own[...] = total.astype(BF16)
+    for r in range(1, n_z):
+        pltpu.make_async_remote_copy(
+            z_own, z_in.at[r - 1], z_send, z_recv, device_id=along_z(r), device_id_type=MESH
         ).start()
 
     @pl.loop(0, n_pos // 128)
@@ -99,19 +119,16 @@
     extra = jnp.where(kind == 0, 1.0, jnp.where(kind == 1, col, jnp.where(kind == 2, line, 0.0)))
     keys_t[pl.ds(ch, 16), :] = extra.astype(BF16)
 
-    all_rs = pltpu.make_async_remote_copy(
-        contrib.at[pl.ds(0, group - 1)], rs_in, rs_send, rs_recv,
-        device_id=peer(1), device_id_type=MESH,
-    )
-    all_rs.wait_recv()
-    total = contrib[me].astype(F32) + jnp.sum(rs_in[...].astype(F32), axis=0)
+    all_z = pltpu.make_async_remote_copy(
+        z_in, z_in, z_send, z_recv, device_id=along_z(1), device_id_type=MESH
+    )
+    all_z.wait_recv()
+    total = total + jnp.sum(z_in[...].astype(F32), axis=0)
     q_own[...] = total.astype(BF16)
     q_all[me] = total.astype(BF16)
-
-    @pl.loop(1, group)
-    def _(r):
+    for r in range(1, plane):
         pltpu.make_async_remote_copy(
-            q_own, q_all.at[me], ag_send, ag_recv, device_id=peer(r), device_id_type=MESH
+            q_own, q_all.at[me], ag_send, ag_recv, device_id=in_plane(r)[1], device_id_type=MESH
         ).start()
 
     eye = lax.broadcasted_iota(jnp.int32, (ch, ch), 0) == lax.broadcasted_iota(
@@ -134,16 +151,18 @@
         proj[frame] = gain
 
     all_ag = pltpu.make_async_remote_copy(
-        rs_in, rs_in, ag_send, ag_recv, device_id=peer(1), device_id_type=MESH
+        rs_in, rs_in, ag_send, ag_recv, device_id=in_plane(1)[1], device_id_type=MESH
     )
     all_ag.wait_recv()
-    q_t[...] = q_all[...].astype(F32).reshape(n_q, ch).T.astype(BF16)
+    scaled = (q_all[...].astype(F32).reshape(n_q, ch) * (math.log2(math.e) / math.sqrt(ch))).T
+    high = scaled.astype(BF16)
+    q_t[pl.ds(0, ch), :] = high
+    q_t[pl.ds(ch, ch), :] = (scaled - high.astype(F32)).astype(BF16)
 
     half = n_q // 2
     pair = lax.div(y, 2)
-    scale = math.log2(math.e) / math.sqrt(ch)
-    t1 = 768
-    t2 = 1536
+    tile = 768
+    n_tiles = n_pos // tile
 
     def part_copy(slot, to):
         return pltpu.make_async_remote_copy(
@@ -151,27 +170,53 @@
             device_id={"space": to}, device_id_type=MESH,
         )
 
+    def score(buf, j, q_at):
+        k = keys[pl.ds(pl.multiple_of(j * tile, tile), tile), :]
+        s = jnp.dot(
+            jnp.concatenate([k, k], axis=1), q_t[:, pl.ds(q_at, half)],
+            preferred_element_type=F32,
+        )
+        buf[...] = s
+        return jnp.max(jnp.max(s.reshape(tile // 8, 8, half), axis=0), axis=0, keepdims=True)
+
+    def gather(buf, j, top, fade):
+        e = jnp.exp2(buf[...] - top).astype(BF16)
+        at = pl.multiple_of(j * tile, tile)
+        acc[...] = acc[...] * fade + jnp.dot(
+            keys_t[:, pl.ds(at, tile)], e, preferred_element_type=F32
+        )
+
+    def raised(top, seen):
+        higher = jnp.maximum(top, seen)
+        return higher, jnp.exp2(top - higher)
+
+    q_ats = [
+        pl.multiple_of((1 - pair) * half, half), pl.multiple_of(pair * half, half)
+    ]
+    top = score(even, 0, q_ats[0])
     for chunk in range(2):
         which = (1 - pair) if chunk == 0 else pair
-        q_at = pl.multiple_of(which * half, half)
-
-        def first(j, top):
-            at = pl.multiple_of(j * t1, t1)
-            s = jnp.dot(
-                keys[pl.ds(at, t1), :], q_t[:, pl.ds(q_at, half)], preferred_element_type=F32
-            )
-            scores[pl.ds(at, t1), :] = s
-            return jnp.maximum(top, jnp.max(s.reshape(t1 // 8, 8, half), axis=0))
-
-        top = lax.fori_loop(0, n_pos // t1, first, jnp.full((8, half), -jnp.inf, F32))
-        top = jnp.max(top, axis=0, keepdims=True)
+        q_at = q_ats[chunk]
         acc[...] = jnp.zeros_like(acc)
 
-        @pl.loop(0, n_pos // t2)
-        def _(j):
-            at = pl.multiple_of(j * t2, t2)
-            e = jnp.exp2((scores[pl.ds(at, t2), :] - top) * scale).astype(BF16)
-            acc[...] += jnp.dot(keys_t[:, pl.ds(at, t2)], e, preferred_element_type=F32)
+        def two(i, carry):
+            top, fade = carry
+            seen = score(odd, 2 * i + 1, q_at)
+            gather(even, 2 * i, top, fade)
+            top, fade = raised(top, seen)
+            seen = score(even, 2 * i + 2, q_at)
+            gather(odd, 2 * i + 1, top, fade)
+            return raised(top, seen)
+
+        top, fade = lax.fori_loop(
+            0, n_tiles // 2 - 1, two, (top, jnp.ones((1, half), F32))
+        )
+        seen = score(odd, n_tiles - 1, q_at)
+        gather(even, n_tiles - 2, top, fade)
+        top, fade = raised(top, seen)
+        if chunk == 0:
+            next_top = score(even, 0, q_ats[1])
+        gather(odd, n_tiles - 1, top, fade)
 
         for side in range(2):
             to = which * 2 + side
@@ -187,6 +232,9 @@
                 def _():
                     part_copy(slot, to).start()
 
+        if chunk == 0:
+            top = next_top
+
     for slot in range(1, n_sp):
         part_copy(slot, y).wait_recv()
     own = part[0]
@@ -195,7 +243,7 @@
     best = functools.reduce(jnp.maximum, tops)
     mixed = None
     for p, m in zip(parts, tops):
-        v = p[: ch + 8] * jnp.exp2((m - best) * scale)
+        v = p[: ch + 8] * jnp.exp2(m - best)
         mixed = v if mixed is None else mixed + v
     inverse = 1.0 / mixed[ch : ch + 1]
     position = mixed[ch + 1 : ch + 3] * inverse
@@ -229,31 +277,55 @@
         precision=lax.Precision.HIGHEST,
     )
     term[...] = terms.reshape(n_tm, 2, q_blk)
-    term[t] = term[t] + position
-    term_in[me] = term[t]
-
-    @pl.loop(1, group)
-    def _(r):
-        other = peer(r)
+
+    def term_copy(source, target, slot):
+        return pltpu.make_async_remote_copy(
+            term.at[target], term_in.at[source], term_send.at[slot], term_recv.at[source],
+            device_id={"tm": target}, device_id_type=MESH,
+        )
+
+    for r in range(1, n_tm):
+
+        @pl.when(t + r < n_tm)
+        def _():
+            term_copy(t, t + r, r).start()
+
+    for source in range(n_tm - 1):
+
+        @pl.when(source < t)
+        def _():
+            term_copy(source, t, 0).wait_recv()
+
+    track = term[t] + position
+    for source in range(n_tm - 1):
+        track = track + jnp.where(source < t, term_in[source], 0.0)
+    row_own[...] = track
+    row_all[y] = track
+    for r in range(1, n_sp):
         pltpu.make_async_remote_copy(
-            term.at[other["tm"]], term_in.at[me], term_send, term_recv,
-            device_id=other, device_id_type=MESH,
+            row_own, row_all.at[y], row_send, row_recv,
+            device_id={"space": lax.rem(y + r, n_sp)}, device_id_type=MESH,
         ).start()
-
-    all_term = pltpu.make_async_remote_copy(
-        term_in.at[pl.ds(0, group - 1)], term_in.at[pl.ds(0, group - 1)], term_send, term_recv,
-        device_id=peer(1), device_id_type=MESH,
-    )
-    all_term.wait()
+    all_row = pltpu.make_async_remote_copy(
+        row_all.at[pl.ds(0, n_sp - 1)], row_all.at[pl.ds(0, n_sp - 1)], row_send, row_recv,
+        device_id={"space": lax.rem(y + 1, n_sp)}, device_id_type=MESH,
+    )
+    all_row.wait()
     for b in range(n_sp):
-        out[:, b * q_blk : (b + 1) * q_blk] = jnp.sum(term_in[pl.ds(b * n_tm, n_tm)], axis=0)
+        out[:, b * q_blk : (b + 1) * q_blk] = row_all[b]
 
     all_rs.wait_send()
+    all_z.wait_send()
     all_ag.wait_send()
     for slot in range(1, n_sp):
         part_copy(slot, y).wait_send()
     halo(0).wait_send()
     halo(1).wait_send()
+    for r in range(1, n_tm):
+
+        @pl.when(t + r < n_tm)
+        def _():
+            term_copy(t, t + r, r).wait_send()
 
 
 def solution(mesh):
@@ -263,8 +335,9 @@
         frames, rows, width, ch = fm.shape
         n_q = q_frame.shape[0]
         n_pos = rows * width
-        group = n_tm * n_sp
-        per_home = n_q // group
+        plane = 2 * n_sp
+        n_z = n_tm // 2
+        home = n_q // plane
         q_blk = n_q // n_sp
         half = n_q // 2
         dims = (n_tm, n_sp, n_q, rows, width, ch, rows * n_sp)
@@ -281,25 +354,31 @@
                 pltpu.VMEM((n_pos + 8, ch), F32),
                 pltpu.VMEM((ch + 16, n_pos), BF16),
                 pltpu.VMEM((n_q, ch), F32),
-                pltpu.VMEM((group, per_home, ch), BF16),
-                pltpu.VMEM((group - 1, per_home, ch), BF16),
-                pltpu.VMEM((per_home, ch), BF16),
-                pltpu.VMEM((group, per_home, ch), BF16),
-                pltpu.VMEM((ch, n_q), BF16),
+                pltpu.VMEM((plane, home, ch), BF16),
+                pltpu.VMEM((plane - 1, home, ch), BF16),
+                pltpu.VMEM((home, ch), BF16),
+                pltpu.VMEM((n_z - 1, home, ch), BF16),
+                pltpu.VMEM((home, ch), BF16),
+                pltpu.VMEM((plane, home, ch), BF16),
+                pltpu.VMEM((2 * ch, n_q), BF16),
                 pltpu.VMEM((n_tm, 1, ch), F32),
                 pltpu.VMEM((3, ch, q_blk), F32),
                 pltpu.VMEM((ch, ch), BF16),
                 pltpu.VMEM((n_tm, 2, ch), F32),
-                pltpu.VMEM((n_pos, half), F32),
+                pltpu.VMEM((768, half), F32),
+                pltpu.VMEM((768, half), F32),
                 pltpu.VMEM((ch + 16, half), F32),
                 pltpu.VMEM((n_sp, ch + 16, q_blk), F32),
                 pltpu.VMEM((n_sp - 1, ch + 16, q_blk), F32),
                 pltpu.VMEM((ch, q_blk), BF16),
                 pltpu.VMEM((2, ch, q_blk), BF16),
                 pltpu.VMEM((n_tm, 2, q_blk), F32),
-                pltpu.VMEM((group, 2, q_blk), F32),
-                dma, dma, dma, dma, dma, dma, dma,
-                dma((n_sp - 1,)), dma((n_sp - 1,)), dma((2,)), dma((2,)), dma, dma,
+                pltpu.VMEM((n_tm - 1, 2, q_blk), F32),
+                pltpu.VMEM((2, q_blk), F32),
+                pltpu.VMEM((n_sp, 2, q_blk), F32),
+                dma, dma, dma, dma, dma, dma, dma, dma, dma,
+                dma((n_sp - 1,)), dma((n_sp - 1,)), dma((2,)), dma((2,)),
+                dma((n_tm,)), dma((n_tm - 1,)), dma, dma,
             ],
             compiler_params=pltpu.CompilerParams(collective_id=0, has_side_effects=True),
         )(fm.reshape(n_pos, ch), q_frame, q_row, q_col, decay, taps, pw, out_w)

time: 51.7 us -> 45.7 us (0.88)
  Pallas kernels: 50.2 us -> 43.8 us
    pallas_call x1, Pallas kernels: 50.2 us -> 43.8 us  [local(): pl.pallas_call(functools.partial(kernel, dims), out_shape=jax.ShapeDtypeS...]
where the time goes in v2:
time: 45.7 us; the launch traced here: 45.1 us
  Pallas kernels  43.8 us (96%)
  local copies, waits for them, and re-layouts  1.28 us (3%)
    pallas_call x1, Pallas kernels, local(): pl.pallas_call(functools.partial(kernel, dims), out_shape=jax.ShapeDtypeS...  43.8 us
    unnamed x1, local copies, waits for them, and re-layouts  1.28 us

profile of v2, /device:TPU:1, one launch (start us, length us, event | category | flops | bytes accessed | tf_op | source)
XLA Modules:
  0.0 45.1 jit_solution(895435689365782888)
XLA Ops:
  0.0 43.8 %shard_map.82 = f32[2,512]{1,0:T(2,128)} custom-call(bf16[7680,128]{1,0:T(8,128)(2,1)} %bitcast.2, s32[512]{0:T(512)} %q_frame.1, s32[512]{0:T(512)} %q_row.1, s32[512]{0:T(512)} %q_col.1, f32[1,128]{1,0:T(1,128)} %decay.1, f32[3,128]{1,0:T(4,128)} %taps.1, bf16[128,128]{1,0:T(8,128)(2,1)} %pw.1, f32[2,128]{1,0:T(2,128)} %out_w.1), custom_call_target="tpu_custom_call" | custom-call | tf_op jit(solution)/shard_map/pallas_call | solution.py:347
  43.8 1.3 %copy.10 = f32[1,2,512]{2,1,0:T(2,128)} copy(f32[1,2,512]{2,1,0:T(2,128)} %bitcast.3) | data formatting | bytes 8192

commit v3 on v2

v3 whole, which is shorter than its diff:
```python
import functools
import math

import jax
import jax.numpy as jnp
from jax import lax
from jax.experimental import pallas as pl
from jax.experimental.pallas import tpu as pltpu
from jax.sharding import PartitionSpec as P

MESH = pl.DeviceIdType.MESH
F32 = jnp.float32
BF16 = jnp.bfloat16


def far_first(n):
    return sorted(range(1, n), key=lambda r: -min(r, n - r))


def kernel(
    dims, fm, q_frame, q_row, q_col, decay, taps, pw, out_w, out,
    rows_v, rows_s, keys, keys32, keys_t, contrib32, contrib, rs_in, z_own, z_in, q_own, q_all, q_t, decay_all,
    tap_cols, pw_t, proj, even, odd, acc, part, part_in, att_own, att_in, term, term_in,
    key_sem, row_sem, rs_send, rs_recv, z_send, z_recv, ag_send, ag_recv, dec_send, dec_recv,
    part_send, part_recv, halo_send, halo_recv, term_send, term_recv,
):
    n_tm, n_sp, n_q, rows, width, ch, height = dims
    n_z = n_tm // 2
    plane = 2 * n_sp
    q_blk = n_q // n_sp
    n_pos = rows * width
    t = lax.axis_index("tm")
    y = lax.axis_index("space")
    z = lax.div(t, 2)
    core = lax.rem(t, 2)
    me = y * 2 + core

    def in_plane(r):
        other = lax.rem(me + r, plane)
        return other, {"tm": z * 2 + lax.rem(other, 2), "space": lax.div(other, 2)}

    def along_z(r):
        return {"tm": lax.rem(t + 2 * r, n_tm)}

    n_loads = 4
    piece = n_pos // n_loads

    def load(i):
        cut = pl.ds(i * piece, piece)
        return pltpu.make_async_copy(fm.at[cut], keys.at[cut], key_sem.at[i])

    for i in range(n_loads):
        load(i).start()
    line = q_frame[...] * height + q_row[...] - (t * height + y * rows)
    mine = (line >= 0) & (line < rows)
    rows_v[...] = jnp.where(mine, line * width + q_col[...], n_pos)
    tell = pltpu.make_async_copy(rows_v, rows_s, row_sem)
    tell.start()
    barrier = pltpu.get_barrier_semaphore()
    for r in range(1, n_tm):
        pl.semaphore_signal(
            barrier, inc=1, device_id={"tm": lax.rem(t + r, n_tm)}, device_id_type=MESH
        )
    for r in range(1, n_sp):
        for c in range(2):
            pl.semaphore_signal(
                barrier, inc=1, device_id={"tm": z * 2 + c, "space": lax.rem(y + r, n_sp)},
                device_id_type=MESH,
            )
    step = 384
    keys32[pl.ds(n_pos, 8), :] = jnp.zeros((8, ch), F32)
    for i in range(n_loads):
        load(i).wait()

        @pl.loop(0, piece // step)
        def _(j):
            at = pl.multiple_of(i * piece + j * step, step)
            keys32[pl.ds(at, step), :] = keys[pl.ds(at, step), :].astype(F32)

    tell.wait()
    for b in range(n_q // 128):

        @pl.loop(0, 8)
        def _(i):
            for u in range(16):
                at = rows_s[b, i * 16 + u]
                contrib32[pl.ds(b * 128 + i * 16 + u, 1), :] = keys32[pl.ds(at, 1), :]

    contrib[...] = contrib32[...].reshape(plane, n_q // plane, ch).astype(BF16)

    pl.semaphore_wait(barrier, n_tm - 1 + plane - 2)

    def rs_copy(r):
        other, device = in_plane(r)
        return pltpu.make_async_remote_copy(
            contrib.at[other], rs_in.at[r - 1], rs_send, rs_recv,
            device_id=device, device_id_type=MESH,
        )

    for r in far_first(plane):
        rs_copy(r).start()

    decay_all[t] = decay[...]

    @pl.loop(1, n_tm)
    def _(r):
        pltpu.make_async_remote_copy(
            decay, decay_all.at[t], dec_send, dec_recv,
            device_id={"tm": lax.rem(t + r, n_tm)}, device_id_type=MESH,
        ).start()

    all_rs = pltpu.make_async_remote_copy(
        rs_in, rs_in, rs_send, rs_recv, device_id=in_plane(1)[1], device_id_type=MESH
    )
    all_rs.wait_recv()
    total = contrib[me].astype(F32) + jnp.sum(rs_in[...].astype(F32), axis=0)
    z_own[...] = total.astype(BF16)
    for r in far_first(n_z):
        pltpu.make_async_remote_copy(
            z_own, z_in.at[r - 1], z_send, z_recv, device_id=along_z(r), device_id_type=MESH
        ).start()

    @pl.loop(0, n_pos // 128)
    def _(j):
        at = pl.multiple_of(j * 128, 128)
        keys_t[pl.ds(0, ch), pl.ds(at, 128)] = keys32[pl.ds(at, 128), :].T.astype(BF16)

    place = lax.broadcasted_iota(jnp.int32, (16, n_pos), 1).astype(F32)
    line = jnp.floor((place + 0.5) * (1.0 / width))
    col = place - line * width
    line = line + (y * rows).astype(F32)
    kind = lax.broadcasted_iota(jnp.int32, (16, n_pos), 0)
    extra = jnp.where(kind == 0, 1.0, jnp.where(kind == 1, col, jnp.where(kind == 2, line, 0.0)))
    keys_t[pl.ds(ch, 16), :] = extra.astype(BF16)

    all_z = pltpu.make_async_remote_copy(
        z_in, z_in, z_send, z_recv, device_id=along_z(1), device_id_type=MESH
    )
    all_z.wait_recv()
    total = total + jnp.sum(z_in[...].astype(F32), axis=0)
    q_own[...] = total.astype(BF16)
    q_all[me] = total.astype(BF16)
    for r in far_first(plane):
        pltpu.make_async_remote_copy(
            q_own, q_all.at[me], ag_send, ag_recv, device_id=in_plane(r)[1], device_id_type=MESH
        ).start()

    eye = lax.broadcasted_iota(jnp.int32, (ch, ch), 0) == lax.broadcasted_iota(
        jnp.int32, (ch, ch), 1
    )
    for k in range(3):
        column = jnp.sum(jnp.where(eye, taps[pl.ds(k, 1), :], 0.0), axis=1, keepdims=True)
        tap_cols[k] = jnp.broadcast_to(column, (ch, q_blk))
    pw_t[...] = pw[...].astype(F32).T.astype(BF16)
    all_dec = pltpu.make_async_remote_copy(
        decay_all.at[pl.ds(0, n_tm - 1)], decay_all.at[pl.ds(0, n_tm - 1)], dec_send, dec_recv,
        device_id={"tm": lax.rem(t + 1, n_tm)}, device_id_type=MESH,
    )
    all_dec.wait()
    run = out_w[...] * (1.0 - decay[...])
    gain = jnp.zeros_like(run)
    for frame in range(n_tm):
        kept = gain if frame == 0 else gain * decay_all[frame]
        gain = jnp.where(t == frame, run, jnp.where(t < frame, kept, 0.0))
        proj[frame] = gain

    all_ag = pltpu.make_async_remote_copy(
        rs_in, rs_in, ag_send, ag_recv, device_id=in_plane(1)[1], device_id_type=MESH
    )
    all_ag.wait_recv()
    q_t[...] = q_all[...].astype(F32).reshape(n_q, ch).T.astype(BF16)

    half = n_q // 2
    pair = lax.div(y, 2)
    scale = math.log2(math.e) / math.sqrt(ch)

    def part_copy(slot, to):
        return pltpu.make_async_remote_copy(
            part.at[slot], part_in.at[slot - 1], part_send.at[slot - 1], part_recv.at[slot - 1],
            device_id={"space": to}, device_id_type=MESH,
        )

    def score(buf, at, size, q_at):
        s = jnp.dot(
            keys[pl.ds(at, size), :], q_t[:, pl.ds(q_at, half)], preferred_element_type=F32
        )
        buf[pl.ds(at, size), :] = s
        return jnp.max(s.reshape(size // 8, 8, half), axis=0)

    def weigh(buf, at, size, top):
        e = jnp.exp2((buf[pl.ds(at, size), :] - top) * scale).astype(BF16)
        acc[...] += jnp.dot(keys_t[:, pl.ds(at, size)], e, preferred_element_type=F32)

    def hand_over(which, top, last):
        for side in range(2):
            to = which * 2 + side
            slot = lax.rem(to - y + n_sp, n_sp)
            lanes = slice(side * q_blk, (side + 1) * q_blk)
            part[slot, pl.ds(0, ch + 8), :] = acc[pl.ds(0, ch + 8), lanes]
            part[slot, pl.ds(ch + 8, 8), :] = jnp.broadcast_to(top[:, lanes], (8, q_blk))
            if last:

                @pl.when(slot != 0)
                def _():
                    part_copy(slot, to).start()
            else:
                part_copy(slot, to).start()

    far, near = 1 - pair, pair
    step_both, step_last = n_pos // 3, n_pos // 2
    top_far = score(even, 0, n_pos, pl.multiple_of(far * half, half))
    top_far = jnp.max(top_far, axis=0, keepdims=True)
    acc[...] = jnp.zeros_like(acc)

    def both(j, top):
        at = pl.multiple_of(j * step_both, step_both)
        top = jnp.maximum(top, score(odd, at, step_both, pl.multiple_of(near * half, half)))
        weigh(even, at, step_both, top_far)
        return top

    top_near = lax.fori_loop(0, 3, both, jnp.full((8, half), -jnp.inf, F32))
    top_near = jnp.max(top_near, axis=0, keepdims=True)
    hand_over(far, top_far, False)
    acc[...] = jnp.zeros_like(acc)

    @pl.loop(0, 2)
    def _(j):
        weigh(odd, pl.multiple_of(j * step_last, step_last), step_last, top_near)

    hand_over(near, top_near, True)

    for slot in range(1, n_sp):
        part_copy(slot, y).wait_recv()
    own = part[0]
    parts = [own] + [part_in[i] for i in range(n_sp - 1)]
    tops = [p[ch + 8 : ch + 9] for p in parts]
    best = functools.reduce(jnp.maximum, tops)
    mixed = None
    for p, m in zip(parts, tops):
        v = p[: ch + 8] * jnp.exp2((m - best) * scale)
        mixed = v if mixed is None else mixed + v
    inverse = 1.0 / mixed[ch : ch + 1]
    position = mixed[ch + 1 : ch + 3] * inverse
    unit = jnp.where(
        lax.broadcasted_iota(jnp.int32, (2, q_blk), 0) == 0, 1.0 / width, 1.0 / height
    )
    position = position * unit
    att = (mixed[:ch] * inverse).astype(BF16)
    att_own[...] = att

    def halo(side):
        to = lax.rem(t + (1 if side == 0 else n_tm - 1), n_tm)
        return pltpu.make_async_remote_copy(
            att_own, att_in.at[side], halo_send.at[side], halo_recv.at[side],
            device_id={"tm": to}, device_id_type=MESH,
        )

    halo(0).start()
    halo(1).start()
    att = att.astype(F32)
    mid = att * tap_cols[1]
    halo(0).wait_recv()
    halo(1).wait_recv()
    before = jnp.where(t > 0, att_in[0].astype(F32), 0.0)
    after = jnp.where(t < n_tm - 1, att_in[1].astype(F32), 0.0)
    depth = tap_cols[0] * before + mid + tap_cols[2] * after
    hidden = jax.nn.gelu(depth).astype(BF16)
    refined = att + jnp.dot(pw_t[...], hidden, preferred_element_type=F32)
    terms = jnp.dot(
        proj[...].reshape(2 * n_tm, ch), refined, preferred_element_type=F32,
        precision=lax.Precision.HIGHEST,
    )
    term[...] = terms.reshape(n_tm, 2, q_blk)

    own = term[t] + position
    term[t] = own
    term_in[t, y] = own

    def term_copy(r, k):
        return pltpu.make_async_remote_copy(
            term.at[t + r], term_in.at[t, y], term_send.at[r], term_recv.at[t],
            device_id={"tm": t + r, "space": lax.rem(y + k, n_sp)}, device_id_type=MESH,
        )

    def terms_of(source, count, slot):
        some = term_in.at[source, pl.ds(0, count)]
        return pltpu.make_async_remote_copy(
            some, some, term_send.at[slot], term_recv.at[source],
            device_id={"space": lax.rem(y + 1, n_sp)}, device_id_type=MESH,
        )

    for k in range(1, n_sp):
        term_copy(0, k).start()
    for r in range(1, n_tm):

        @pl.when(t + r < n_tm)
        def _():
            for k in range(n_sp):
                term_copy(r, k).start()

    for source in range(n_tm - 1):

        @pl.when(source < t)
        def _():
            terms_of(source, n_sp, 0).wait_recv()

    terms_of(t, n_sp - 1, 0).wait()
    for b in range(n_sp):
        track = term_in[t, b]
        for source in range(n_tm - 1):
            track = track + jnp.where(source < t, term_in[source, b], 0.0)
        out[:, b * q_blk : (b + 1) * q_blk] = track

    all_rs.wait_send()
    all_z.wait_send()
    all_ag.wait_send()
    for slot in range(1, n_sp):
        part_copy(slot, y).wait_send()
    halo(0).wait_send()
    halo(1).wait_send()
    for r in range(1, n_tm):

        @pl.when(t + r < n_tm)
        def _():
            terms_of(0, n_sp, r).wait_send()


def solution(mesh):
    n_tm, n_sp = mesh.shape["tm"], mesh.shape["space"]

    def local(fm, q_frame, q_row, q_col, decay, taps, pw, out_w):
        frames, rows, width, ch = fm.shape
        n_q = q_frame.shape[0]
        n_pos = rows * width
        plane = 2 * n_sp
        n_z = n_tm // 2
        home = n_q // plane
        q_blk = n_q // n_sp
        half = n_q // 2
        dims = (n_tm, n_sp, n_q, rows, width, ch, rows * n_sp)
        vmem = pl.BlockSpec(memory_space=pltpu.VMEM)
        dma = pltpu.SemaphoreType.DMA
        queries = [a.reshape(n_q // 128, 128) for a in (q_frame, q_row, q_col)]
        out = pl.pallas_call(
            functools.partial(kernel, dims),
            out_shape=jax.ShapeDtypeStruct((2, n_q), F32),
            in_specs=[pl.BlockSpec(memory_space=pl.ANY)] + [vmem] * 7,
            out_specs=vmem,
            scratch_shapes=[
                pltpu.VMEM((n_q // 128, 128), jnp.int32),
                pltpu.SMEM((n_q // 128, 128), jnp.int32),
                pltpu.VMEM((n_pos, ch), BF16),
                pltpu.VMEM((n_pos + 8, ch), F32),
                pltpu.VMEM((ch + 16, n_pos), BF16),
                pltpu.VMEM((n_q, ch), F32),
                pltpu.VMEM((plane, home, ch), BF16),
                pltpu.VMEM((plane - 1, home, ch), BF16),
                pltpu.VMEM((home, ch), BF16),
                pltpu.VMEM((n_z - 1, home, ch), BF16),
                pltpu.VMEM((home, ch), BF16),
                pltpu.VMEM((plane, home, ch), BF16),
                pltpu.VMEM((ch, n_q), BF16),
                pltpu.VMEM((n_tm, 1, ch), F32),
                pltpu.VMEM((3, ch, q_blk), F32),
                pltpu.VMEM((ch, ch), BF16),
                pltpu.VMEM((n_tm, 2, ch), F32),
                pltpu.VMEM((n_pos, half), F32),
                pltpu.VMEM((n_pos, half), F32),
                pltpu.VMEM((ch + 16, half), F32),
                pltpu.VMEM((n_sp, ch + 16, q_blk), F32),
                pltpu.VMEM((n_sp - 1, ch + 16, q_blk), F32),
                pltpu.VMEM((ch, q_blk), BF16),
                pltpu.VMEM((2, ch, q_blk), BF16),
                pltpu.VMEM((n_tm, 2, q_blk), F32),
                pltpu.VMEM((n_tm, n_sp, 2, q_blk), F32),
                dma((4,)), dma, dma, dma, dma, dma, dma, dma, dma, dma,
                dma((n_sp - 1,)), dma((n_sp - 1,)), dma((2,)), dma((2,)),
                dma((n_tm,)), dma((n_tm,)),
            ],
            compiler_params=pltpu.CompilerParams(collective_id=0, has_side_effects=True),
        )(fm.reshape(n_pos, ch), *queries, decay, taps, pw, out_w)
        return out[None]

    placed = (
        P(("video", "tm"), "space", None, None),
        P("video"),
        P("video"),
        P("video"),
        P(("video", "tm"), None),
        P(),
        P(),
        P(),
    )
    return jax.shard_map(
        local, mesh=mesh, in_specs=placed, out_specs=P(("video", "tm"), None, None), check_vma=False
    )
```

time: 45.7 us -> 41.7 us (0.912)
  Pallas kernels: 43.8 us -> 40.2 us
    pallas_call x1, Pallas kernels: 43.8 us -> 40.2 us  [local(): pl.pallas_call(functools.partial(kernel, dims), out_shape=jax.ShapeDtypeS...]
where the time goes in v3:
time: 41.7 us; the launch traced here: 41.5 us
  Pallas kernels  40.2 us (96%)
  local copies, waits for them, and re-layouts  1.28 us (3%)
    pallas_call x1, Pallas kernels, local(): pl.pallas_call(functools.partial(kernel, dims), out_shape=jax.ShapeDtypeS...  40.2 us
    unnamed x1, local copies, waits for them, and re-layouts  1.28 us

profile of v3, /device:TPU:1, one launch (start us, length us, event | category | flops | bytes accessed | tf_op | source)
XLA Modules:
  0.0 41.5 jit_solution(4040817970729713969)
XLA Ops:
  0.0 40.2 %shard_map.82 = f32[2,512]{1,0:T(2,128)} custom-call(bf16[7680,128]{1,0:T(8,128)(2,1)} %bitcast.5, s32[4,128]{1,0:T(4,128)} %bitcast.7, s32[4,128]{1,0:T(4,128)} %bitcast.8, s32[4,128]{1,0:T(4,128)} %bitcast.9, f32[1,128]{1,0:T(1,128)} %decay.1, f32[3,128]{1,0:T(4,128)} %taps.1, bf16[128,128]{1,0:T(8,128)(2,1)} %pw.1, f32[2,128]{1,0:T(2,128)} %out_w.1), custom_call_target="tpu_custom_call" | custom-call | tf_op jit(solution)/shard_map/pallas_call | solution.py:344
  40.2 1.3 %copy.10 = f32[1,2,512]{2,1,0:T(2,128)} copy(f32[1,2,512]{2,1,0:T(2,128)} %bitcast.6) | data formatting | bytes 8192

commit v4 on v3

--- a/solution.py
+++ b/solution.py
@@ -11,6 +11,7 @@
 MESH = pl.DeviceIdType.MESH
 F32 = jnp.float32
 BF16 = jnp.bfloat16
+SIB = jnp.bfloat16
 
 
 def far_first(n):
@@ -19,10 +20,12 @@
 
 def kernel(
     dims, fm, q_frame, q_row, q_col, decay, taps, pw, out_w, out,
-    rows_v, rows_s, keys, keys32, keys_t, contrib32, contrib, rs_in, z_own, z_in, q_own, q_all, q_t, decay_all,
-    tap_cols, pw_t, proj, even, odd, acc, part, part_in, att_own, att_in, term, term_in,
-    key_sem, row_sem, rs_send, rs_recv, z_send, z_recv, ag_send, ag_recv, dec_send, dec_recv,
-    part_send, part_recv, halo_send, halo_recv, term_send, term_recv,
+    rows_v, rows_s, keys, keys32, keys_t, contrib32, contrib, rs_in, z_own, z_in, q_own, q_all, q_far, q_near, decay_all,
+    tap_cols, pw_t, proj, even, odd, acc_far, acc, part, part_in, sib_out, sib_in, sib_facts,
+    sib_facts_in, att_own, att_in, term, term_in,
+    key_sem, row_sem, rs_send, rs_recv, z_send, z_recv, ag_send, ag_recv, on_send,
+    on_recv, dec_send, dec_recv,
+    part_send, part_recv, sib_send, sib_recv, halo_send, halo_recv, term_send, term_recv,
 ):
     n_tm, n_sp, n_q, rows, width, ch, height = dims
     n_z = n_tm // 2
@@ -140,10 +143,46 @@
     total = total + jnp.sum(z_in[...].astype(F32), axis=0)
     q_own[...] = total.astype(BF16)
     q_all[me] = total.astype(BF16)
-    for r in far_first(plane):
-        pltpu.make_async_remote_copy(
-            q_own, q_all.at[me], ag_send, ag_recv, device_id=in_plane(r)[1], device_id_type=MESH
-        ).start()
+    on_chip = pltpu.make_async_remote_copy(
+        q_own, q_all.at[me], on_send, on_recv, device_id={"tm": t + 1 - 2 * core},
+        device_id_type=MESH,
+    )
+    on_chip.start()
+    for k in far_first(n_sp):
+        for c in range(2):
+            pltpu.make_async_remote_copy(
+                q_own, q_all.at[me], ag_send, ag_recv,
+                device_id={"tm": z * 2 + c, "space": lax.rem(y + k, n_sp)}, device_id_type=MESH,
+            ).start()
+
+    pair = lax.div(y, 2)
+    scale = math.log2(math.e) / math.sqrt(ch)
+
+    def turned(first, count):
+        return q_all[pl.ds(first, count)].astype(F32).reshape(-1, ch).T.astype(BF16)
+
+    def score(buf, q, at, size):
+        s = jnp.dot(keys[pl.ds(at, size), :], q[...], preferred_element_type=F32)
+        buf[pl.ds(at, size), :] = s
+        return jnp.max(s.reshape(size // 8, 8, s.shape[1]), axis=0)
+
+    def weigh(buf, total, at, size, top):
+        e = jnp.exp2((buf[pl.ds(at, size), :] - top) * scale).astype(BF16)
+        total[...] += jnp.dot(keys_t[:, pl.ds(at, size)], e, preferred_element_type=F32)
+
+    step_both, step_last = n_pos // 3, n_pos // 2
+
+    on_chip.wait_recv()
+    q_near[...] = turned(2 * y, 2)
+    top_own = jnp.max(score(odd, q_near, 0, n_pos), axis=0, keepdims=True)
+    acc[...] = jnp.zeros_like(acc)
+
+    @pl.loop(0, 2)
+    def _(j):
+        weigh(odd, acc, pl.multiple_of(j * step_last, step_last), step_last, top_own)
+
+    part[2, pl.ds(0, ch + 8), :] = acc[pl.ds(0, ch + 8), :]
+    part[2, pl.ds(ch + 8, 8), :] = jnp.broadcast_to(top_own, (8, q_blk))
 
     eye = lax.broadcasted_iota(jnp.int32, (ch, ch), 0) == lax.broadcasted_iota(
         jnp.int32, (ch, ch), 1
@@ -165,74 +204,66 @@
         proj[frame] = gain
 
     all_ag = pltpu.make_async_remote_copy(
-        rs_in, rs_in, ag_send, ag_recv, device_id=in_plane(1)[1], device_id_type=MESH
+        q_all.at[pl.ds(0, plane - 2)], q_all.at[pl.ds(0, plane - 2)], ag_send, ag_recv,
+        device_id=in_plane(1)[1], device_id_type=MESH,
     )
     all_ag.wait_recv()
-    q_t[...] = q_all[...].astype(F32).reshape(n_q, ch).T.astype(BF16)
-
-    half = n_q // 2
-    pair = lax.div(y, 2)
-    scale = math.log2(math.e) / math.sqrt(ch)
-
-    def part_copy(slot, to):
-        return pltpu.make_async_remote_copy(
-            part.at[slot], part_in.at[slot - 1], part_send.at[slot - 1], part_recv.at[slot - 1],
-            device_id={"space": to}, device_id_type=MESH,
-        )
-
-    def score(buf, at, size, q_at):
-        s = jnp.dot(
-            keys[pl.ds(at, size), :], q_t[:, pl.ds(q_at, half)], preferred_element_type=F32
-        )
-        buf[pl.ds(at, size), :] = s
-        return jnp.max(s.reshape(size // 8, 8, half), axis=0)
-
-    def weigh(buf, at, size, top):
-        e = jnp.exp2((buf[pl.ds(at, size), :] - top) * scale).astype(BF16)
-        acc[...] += jnp.dot(keys_t[:, pl.ds(at, size)], e, preferred_element_type=F32)
-
-    def hand_over(which, top, last):
-        for side in range(2):
-            to = which * 2 + side
-            slot = lax.rem(to - y + n_sp, n_sp)
-            lanes = slice(side * q_blk, (side + 1) * q_blk)
-            part[slot, pl.ds(0, ch + 8), :] = acc[pl.ds(0, ch + 8), lanes]
-            part[slot, pl.ds(ch + 8, 8), :] = jnp.broadcast_to(top[:, lanes], (8, q_blk))
-            if last:
-
-                @pl.when(slot != 0)
-                def _():
-                    part_copy(slot, to).start()
-            else:
-                part_copy(slot, to).start()
-
-    far, near = 1 - pair, pair
-    step_both, step_last = n_pos // 3, n_pos // 2
-    top_far = score(even, 0, n_pos, pl.multiple_of(far * half, half))
-    top_far = jnp.max(top_far, axis=0, keepdims=True)
-    acc[...] = jnp.zeros_like(acc)
+    far = 1 - pair
+    sib = y + 1 - 2 * lax.rem(y, 2)
+    q_far[...] = turned(4 * far, 4)
+    q_near[...] = turned(2 * sib, 2)
+    top_far = jnp.max(score(even, q_far, 0, n_pos), axis=0, keepdims=True)
+    acc_far[...] = jnp.zeros_like(acc_far)
 
     def both(j, top):
         at = pl.multiple_of(j * step_both, step_both)
-        top = jnp.maximum(top, score(odd, at, step_both, pl.multiple_of(near * half, half)))
-        weigh(even, at, step_both, top_far)
+        top = jnp.maximum(top, score(odd, q_near, at, step_both))
+        weigh(even, acc_far, at, step_both, top_far)
         return top
 
-    top_near = lax.fori_loop(0, 3, both, jnp.full((8, half), -jnp.inf, F32))
-    top_near = jnp.max(top_near, axis=0, keepdims=True)
-    hand_over(far, top_far, False)
+    top_sib = lax.fori_loop(0, 3, both, jnp.full((8, q_blk), -jnp.inf, F32))
+    top_sib = jnp.max(top_sib, axis=0, keepdims=True)
+
+    def part_copy(side):
+        return pltpu.make_async_remote_copy(
+            part.at[side], part_in.at[lax.rem(y, 2)], part_send.at[side],
+            part_recv.at[lax.rem(y, 2)], device_id={"space": far * 2 + side}, device_id_type=MESH,
+        )
+
+    def part_arrival(side):
+        return pltpu.make_async_remote_copy(
+            part.at[side], part_in.at[side], part_send.at[side], part_recv.at[side],
+            device_id={"space": far * 2 + side}, device_id_type=MESH,
+        )
+
+    for side in range(2):
+        lanes = slice(side * q_blk, (side + 1) * q_blk)
+        part[side, pl.ds(0, ch + 8), :] = acc_far[pl.ds(0, ch + 8), lanes]
+        part[side, pl.ds(ch + 8, 8), :] = jnp.broadcast_to(top_far[:, lanes], (8, q_blk))
+        part_copy(side).start()
     acc[...] = jnp.zeros_like(acc)
 
     @pl.loop(0, 2)
     def _(j):
-        weigh(odd, pl.multiple_of(j * step_last, step_last), step_last, top_near)
-
-    hand_over(near, top_near, True)
-
-    for slot in range(1, n_sp):
-        part_copy(slot, y).wait_recv()
-    own = part[0]
-    parts = [own] + [part_in[i] for i in range(n_sp - 1)]
+        weigh(odd, acc, pl.multiple_of(j * step_last, step_last), step_last, top_sib)
+
+    sib_out[...] = acc[pl.ds(0, ch), :].astype(SIB)
+    sib_facts[pl.ds(0, 8), :] = acc[pl.ds(ch, 8), :]
+    sib_facts[pl.ds(8, 8), :] = jnp.broadcast_to(top_sib, (8, q_blk))
+    sib_copies = [
+        pltpu.make_async_remote_copy(
+            a, b, sib_send.at[i], sib_recv.at[i], device_id={"space": sib}, device_id_type=MESH
+        )
+        for i, (a, b) in enumerate([(sib_out, sib_in), (sib_facts, sib_facts_in)])
+    ]
+    for copy in sib_copies:
+        copy.start()
+    for side in range(2):
+        part_arrival(side).wait_recv()
+    for copy in sib_copies:
+        copy.wait_recv()
+    parts = [part[2], part_in[0], part_in[1]]
+    parts.append(jnp.concatenate([sib_in[...].astype(F32), sib_facts_in[...]], axis=0))
     tops = [p[ch + 8 : ch + 9] for p in parts]
     best = functools.reduce(jnp.maximum, tops)
     mixed = None
@@ -314,8 +345,11 @@
     all_rs.wait_send()
     all_z.wait_send()
     all_ag.wait_send()
-    for slot in range(1, n_sp):
-        part_copy(slot, y).wait_send()
+    on_chip.wait_send()
+    for side in range(2):
+        part_copy(side).wait_send()
+    for copy in sib_copies:
+        copy.wait_send()
     halo(0).wait_send()
     halo(1).wait_send()
     for r in range(1, n_tm):
@@ -343,7 +377,7 @@
         queries = [a.reshape(n_q // 128, 128) for a in (q_frame, q_row, q_col)]
         out = pl.pallas_call(
             functools.partial(kernel, dims),
-            out_shape=jax.ShapeDtypeStruct((2, n_q), F32),
+            out_shape=pltpu.VMEM((2, n_q), F32),
             in_specs=[pl.BlockSpec(memory_space=pl.ANY)] + [vmem] * 7,
             out_specs=vmem,
             scratch_shapes=[
@@ -359,22 +393,28 @@
                 pltpu.VMEM((n_z - 1, home, ch), BF16),
                 pltpu.VMEM((home, ch), BF16),
                 pltpu.VMEM((plane, home, ch), BF16),
-                pltpu.VMEM((ch, n_q), BF16),
+                pltpu.VMEM((ch, half), BF16),
+                pltpu.VMEM((ch, q_blk), BF16),
                 pltpu.VMEM((n_tm, 1, ch), F32),
                 pltpu.VMEM((3, ch, q_blk), F32),
                 pltpu.VMEM((ch, ch), BF16),
                 pltpu.VMEM((n_tm, 2, ch), F32),
                 pltpu.VMEM((n_pos, half), F32),
-                pltpu.VMEM((n_pos, half), F32),
+                pltpu.VMEM((n_pos, q_blk), F32),
                 pltpu.VMEM((ch + 16, half), F32),
-                pltpu.VMEM((n_sp, ch + 16, q_blk), F32),
-                pltpu.VMEM((n_sp - 1, ch + 16, q_blk), F32),
+                pltpu.VMEM((ch + 16, q_blk), F32),
+                pltpu.VMEM((3, ch + 16, q_blk), F32),
+                pltpu.VMEM((2, ch + 16, q_blk), F32),
+                pltpu.VMEM((ch, q_blk), SIB),
+                pltpu.VMEM((ch, q_blk), SIB),
+                pltpu.VMEM((16, q_blk), F32),
+                pltpu.VMEM((16, q_blk), F32),
                 pltpu.VMEM((ch, q_blk), BF16),
                 pltpu.VMEM((2, ch, q_blk), BF16),
                 pltpu.VMEM((n_tm, 2, q_blk), F32),
                 pltpu.VMEM((n_tm, n_sp, 2, q_blk), F32),
-                dma((4,)), dma, dma, dma, dma, dma, dma, dma, dma, dma,
-                dma((n_sp - 1,)), dma((n_sp - 1,)), dma((2,)), dma((2,)),
+                dma((4,)), dma, dma, dma, dma, dma, dma, dma, dma, dma, dma, dma,
+                dma((2,)), dma((2,)), dma((2,)), dma((2,)), dma((2,)), dma((2,)),
                 dma((n_tm,)), dma((n_tm,)),
             ],
             compiler_params=pltpu.CompilerParams(collective_id=0, has_side_effects=True),

time: 41.7 us -> 39.6 us (0.950)
  Pallas kernels: 40.2 us -> 38.9 us
  local copies, waits for them, and re-layouts: 1.28 us -> 0.6 us
    pallas_call x1, Pallas kernels: 40.2 us -> 38.9 us  [local(): pl.pallas_call(functools.partial(kernel, dims), out_shape=pltpu.VMEM((2,...]
    unnamed x1, local copies, waits for them, and re-layouts: 1.28 us -> 0.6 us
where the time goes in v4:
time: 39.6 us; the launch traced here: 39.5 us
  Pallas kernels  38.9 us (98%)
  local copies, waits for them, and re-layouts  0.6 us (2%)
    pallas_call x1, Pallas kernels, local(): pl.pallas_call(functools.partial(kernel, dims), out_shape=pltpu.VMEM((2,...  38.9 us

profile of v4, /device:TPU:1, one launch (start us, length us, event | category | flops | bytes accessed | tf_op | source)
XLA Modules:
  0.0 39.5 jit_solution(7345076256791831314)
XLA Ops:
  0.0 38.9 %shard_map.82 = f32[2,512]{1,0:T(2,128)S(1)} custom-call(bf16[7680,128]{1,0:T(8,128)(2,1)} %bitcast.6, s32[4,128]{1,0:T(4,128)} %bitcast.7, s32[4,128]{1,0:T(4,128)} %bitcast.8, s32[4,128]{1,0:T(4,128)} %bitcast.9, f32[1,128]{1,0:T(1,128)} %decay.1, f32[3,128]{1,0:T(4,128)} %taps.1, bf16[128,128]{1,0:T(8,128)(2,1)} %pw.1, f32[2,128]{1,0:T(2,128)} %out_w.1), custom_call_target="tpu_custom_call" | custom-call | tf_op jit(solution)/shard_map/pallas_call | solution.py:378
  38.9 0.6 %copy.10 = f32[1,2,512]{2,1,0:T(2,128)} copy(f32[1,2,512]{2,1,0:T(2,128)S(1)} %bitcast.5) | data formatting | bytes 8192

commit v5 on v4

--- a/solution.py
+++ b/solution.py
@@ -11,7 +11,6 @@
 MESH = pl.DeviceIdType.MESH
 F32 = jnp.float32
 BF16 = jnp.bfloat16
-SIB = jnp.bfloat16
 
 
 def far_first(n):
@@ -19,13 +18,12 @@
 
 
 def kernel(
-    dims, fm, q_frame, q_row, q_col, decay, taps, pw, out_w, out,
-    rows_v, rows_s, keys, keys32, keys_t, contrib32, contrib, rs_in, z_own, z_in, q_own, q_all, q_far, q_near, decay_all,
-    tap_cols, pw_t, proj, even, odd, acc_far, acc, part, part_in, sib_out, sib_in, sib_facts,
-    sib_facts_in, att_own, att_in, term, term_in,
-    key_sem, row_sem, rs_send, rs_recv, z_send, z_recv, ag_send, ag_recv, on_send,
+    dims, fm, q_frame, q_row, q_col, decay_hbm, taps_hbm, pw_hbm, out_w_hbm, out,
+    asked, decay, taps, pw, out_w, rows_v, rows_s, keys, keys32, keys_t, contrib32, contrib, rs_in, z_own, z_in, q_own, q_all, q_far, q_near, decay_all,
+    tap_cols, pw_t, proj, even, odd, acc_far, acc, own_part, feats, feats_in, facts, facts_in, att_own, att_in, term, term_in,
+    ask_sem, small_sem, key_sem, row_sem, rs_send, rs_recv, z_send, z_recv, ag_send, ag_recv, on_send,
     on_recv, dec_send, dec_recv,
-    part_send, part_recv, sib_send, sib_recv, halo_send, halo_recv, term_send, term_recv,
+    feat_send, feat_recv, fact_send, fact_recv, halo_send, halo_recv, term_send, term_recv,
 ):
     n_tm, n_sp, n_q, rows, width, ch, height = dims
     n_z = n_tm // 2
@@ -52,13 +50,22 @@
         cut = pl.ds(i * piece, piece)
         return pltpu.make_async_copy(fm.at[cut], keys.at[cut], key_sem.at[i])
 
+    asks = [
+        pltpu.make_async_copy(a, asked.at[i], ask_sem.at[i])
+        for i, a in enumerate([q_frame, q_row, q_col])
+    ]
+    smalls = [
+        pltpu.make_async_copy(a, b, small_sem.at[i])
+        for i, (a, b) in enumerate(
+            [(decay_hbm, decay), (taps_hbm, taps), (pw_hbm, pw), (out_w_hbm, out_w)]
+        )
+    ]
+    for copy in asks:
+        copy.start()
     for i in range(n_loads):
         load(i).start()
-    line = q_frame[...] * height + q_row[...] - (t * height + y * rows)
-    mine = (line >= 0) & (line < rows)
-    rows_v[...] = jnp.where(mine, line * width + q_col[...], n_pos)
-    tell = pltpu.make_async_copy(rows_v, rows_s, row_sem)
-    tell.start()
+    for copy in smalls:
+        copy.start()
     barrier = pltpu.get_barrier_semaphore()
     for r in range(1, n_tm):
         pl.semaphore_signal(
@@ -70,6 +77,13 @@
                 barrier, inc=1, device_id={"tm": z * 2 + c, "space": lax.rem(y + r, n_sp)},
                 device_id_type=MESH,
             )
+    for copy in asks:
+        copy.wait()
+    line = asked[0] * height + asked[1] - (t * height + y * rows)
+    mine = (line >= 0) & (line < rows)
+    rows_v[...] = jnp.where(mine, line * width + asked[2], n_pos)
+    tell = pltpu.make_async_copy(rows_v, rows_s, row_sem)
+    tell.start()
     step = 384
     keys32[pl.ds(n_pos, 8), :] = jnp.zeros((8, ch), F32)
     for i in range(n_loads):
@@ -81,28 +95,43 @@
             keys32[pl.ds(at, step), :] = keys[pl.ds(at, step), :].astype(F32)
 
     tell.wait()
-    for b in range(n_q // 128):
-
-        @pl.loop(0, 8)
-        def _(i):
+    homes = plane // n_sp
+
+    def rs_sends(k):
+        for c in range(homes):
+            block = lax.rem(y + k, n_sp)
+            there = lax.rem(2 * (n_sp - k) + core - c + plane, plane) - 1
+
+            @pl.when(there >= 0)
+            def _():
+                pltpu.make_async_remote_copy(
+                    contrib.at[block * 2 + c], rs_in.at[there], rs_send, rs_recv,
+                    device_id={"tm": z * 2 + c, "space": block}, device_id_type=MESH,
+                ).start()
+
+    order = far_first(n_sp) + [0]
+    for i, k in enumerate(order):
+        block = lax.rem(y + k, n_sp)
+        first = pl.multiple_of(block * q_blk, q_blk)
+
+        @pl.loop(0, q_blk // 16)
+        def _(j):
             for u in range(16):
-                at = rows_s[b, i * 16 + u]
-                contrib32[pl.ds(b * 128 + i * 16 + u, 1), :] = keys32[pl.ds(at, 1), :]
-
-    contrib[...] = contrib32[...].reshape(plane, n_q // plane, ch).astype(BF16)
-
-    pl.semaphore_wait(barrier, n_tm - 1 + plane - 2)
-
-    def rs_copy(r):
-        other, device = in_plane(r)
-        return pltpu.make_async_remote_copy(
-            contrib.at[other], rs_in.at[r - 1], rs_send, rs_recv,
-            device_id=device, device_id_type=MESH,
-        )
-
-    for r in far_first(plane):
-        rs_copy(r).start()
-
+                at = rows_s[block, j * 16 + u]
+                contrib32[pl.ds(first + j * 16 + u, 1), :] = keys32[pl.ds(at, 1), :]
+
+        contrib[pl.ds(block * 2, 2)] = (
+            contrib32[pl.ds(first, q_blk), :].reshape(2, q_blk // 2, ch).astype(BF16)
+        )
+        if i == 0:
+            pl.semaphore_wait(barrier, n_tm - 1 + plane - 2)
+            for past in order[:i]:
+                rs_sends(past)
+        if i >= 0:
+            rs_sends(k)
+
+    for copy in smalls:
+        copy.wait()
     decay_all[t] = decay[...]
 
     @pl.loop(1, n_tm)
@@ -148,14 +177,14 @@
         device_id_type=MESH,
     )
     on_chip.start()
-    for k in far_first(n_sp):
+    for k in (1, 3, 2):
         for c in range(2):
             pltpu.make_async_remote_copy(
-                q_own, q_all.at[me], ag_send, ag_recv,
+                q_own, q_all.at[me], ag_send.at[k % 2], ag_recv.at[k % 2],
                 device_id={"tm": z * 2 + c, "space": lax.rem(y + k, n_sp)}, device_id_type=MESH,
             ).start()
 
-    pair = lax.div(y, 2)
+    odd_row = lax.rem(y, 2)
     scale = math.log2(math.e) / math.sqrt(ch)
 
     def turned(first, count):
@@ -181,8 +210,7 @@
     def _(j):
         weigh(odd, acc, pl.multiple_of(j * step_last, step_last), step_last, top_own)
 
-    part[2, pl.ds(0, ch + 8), :] = acc[pl.ds(0, ch + 8), :]
-    part[2, pl.ds(ch + 8, 8), :] = jnp.broadcast_to(top_own, (8, q_blk))
+    own_part[...] = acc[pl.ds(0, ch + 8), :]
 
     eye = lax.broadcasted_iota(jnp.int32, (ch, ch), 0) == lax.broadcasted_iota(
         jnp.int32, (ch, ch), 1
@@ -203,17 +231,22 @@
         gain = jnp.where(t == frame, run, jnp.where(t < frame, kept, 0.0))
         proj[frame] = gain
 
-    all_ag = pltpu.make_async_remote_copy(
-        q_all.at[pl.ds(0, plane - 2)], q_all.at[pl.ds(0, plane - 2)], ag_send, ag_recv,
-        device_id=in_plane(1)[1], device_id_type=MESH,
-    )
-    all_ag.wait_recv()
-    far = 1 - pair
-    sib = y + 1 - 2 * lax.rem(y, 2)
-    q_far[...] = turned(4 * far, 4)
-    q_near[...] = turned(2 * sib, 2)
+    def ag_of(k):
+        some = q_all.at[pl.ds(0, 2 + 2 * k)]
+        return pltpu.make_async_remote_copy(
+            some, some, ag_send.at[k], ag_recv.at[k],
+            device_id=in_plane(1)[1], device_id_type=MESH,
+        )
+
+    ag_of(1).wait_recv()
+    sib = lax.rem(y + 2, n_sp)
+    for side in range(2):
+        lanes = slice(side * q_blk, (side + 1) * q_blk)
+        q_far[:, lanes] = turned(2 * (1 - odd_row) + 4 * side, 2)
     top_far = jnp.max(score(even, q_far, 0, n_pos), axis=0, keepdims=True)
     acc_far[...] = jnp.zeros_like(acc_far)
+    ag_of(0).wait_recv()
+    q_near[...] = turned(2 * sib, 2)
 
     def both(j, top):
         at = pl.multiple_of(j * step_both, step_both)
@@ -224,51 +257,48 @@
     top_sib = lax.fori_loop(0, 3, both, jnp.full((8, q_blk), -jnp.inf, F32))
     top_sib = jnp.max(top_sib, axis=0, keepdims=True)
 
-    def part_copy(side):
-        return pltpu.make_async_remote_copy(
-            part.at[side], part_in.at[lax.rem(y, 2)], part_send.at[side],
-            part_recv.at[lax.rem(y, 2)], device_id={"space": far * 2 + side}, device_id_type=MESH,
-        )
-
-    def part_arrival(side):
-        return pltpu.make_async_remote_copy(
-            part.at[side], part_in.at[side], part_send.at[side], part_recv.at[side],
-            device_id={"space": far * 2 + side}, device_id_type=MESH,
-        )
+    def hand_over(slot, to, there, sums, top):
+        feats[slot] = sums[:ch].astype(BF16)
+        facts[slot, pl.ds(0, 8), :] = sums[ch:]
+        facts[slot, pl.ds(8, 8), :] = jnp.broadcast_to(top, (8, q_blk))
+        for copy in part_copies(slot, to, there):
+            copy.start()
+
+    def part_copies(slot, to, there):
+        return [
+            pltpu.make_async_remote_copy(
+                source.at[slot], target.at[there], send.at[slot], recv.at[there],
+                device_id={"space": to}, device_id_type=MESH,
+            )
+            for source, target, send, recv in [
+                (facts, facts_in, fact_send, fact_recv), (feats, feats_in, feat_send, feat_recv)
+            ]
+        ]
 
     for side in range(2):
         lanes = slice(side * q_blk, (side + 1) * q_blk)
-        part[side, pl.ds(0, ch + 8), :] = acc_far[pl.ds(0, ch + 8), lanes]
-        part[side, pl.ds(ch + 8, 8), :] = jnp.broadcast_to(top_far[:, lanes], (8, q_blk))
-        part_copy(side).start()
+        hand_over(
+            side, 1 - odd_row + 2 * side, lax.div(y, 2), acc_far[pl.ds(0, ch + 8), lanes],
+            top_far[:, lanes],
+        )
     acc[...] = jnp.zeros_like(acc)
 
     @pl.loop(0, 2)
     def _(j):
         weigh(odd, acc, pl.multiple_of(j * step_last, step_last), step_last, top_sib)
 
-    sib_out[...] = acc[pl.ds(0, ch), :].astype(SIB)
-    sib_facts[pl.ds(0, 8), :] = acc[pl.ds(ch, 8), :]
-    sib_facts[pl.ds(8, 8), :] = jnp.broadcast_to(top_sib, (8, q_blk))
-    sib_copies = [
-        pltpu.make_async_remote_copy(
-            a, b, sib_send.at[i], sib_recv.at[i], device_id={"space": sib}, device_id_type=MESH
-        )
-        for i, (a, b) in enumerate([(sib_out, sib_in), (sib_facts, sib_facts_in)])
-    ]
-    for copy in sib_copies:
-        copy.start()
-    for side in range(2):
-        part_arrival(side).wait_recv()
-    for copy in sib_copies:
-        copy.wait_recv()
-    parts = [part[2], part_in[0], part_in[1]]
-    parts.append(jnp.concatenate([sib_in[...].astype(F32), sib_facts_in[...]], axis=0))
-    tops = [p[ch + 8 : ch + 9] for p in parts]
-    best = functools.reduce(jnp.maximum, tops)
+    hand_over(2, sib, 2, acc[pl.ds(0, ch + 8), :], top_sib)
+    parts = [(own_part[...], top_own)]
+    for slot in range(3):
+        for copy in part_copies(slot, sib, slot):
+            copy.wait_recv()
+    for slot in range(3):
+        sums = jnp.concatenate([feats_in[slot].astype(F32), facts_in[slot, pl.ds(0, 8), :]], axis=0)
+        parts.append((sums, facts_in[slot, pl.ds(8, 1), :]))
+    best = functools.reduce(jnp.maximum, [top for _, top in parts])
     mixed = None
-    for p, m in zip(parts, tops):
-        v = p[: ch + 8] * jnp.exp2((m - best) * scale)
+    for sums, top in parts:
+        v = sums * jnp.exp2((top - best) * scale)
         mixed = v if mixed is None else mixed + v
     inverse = 1.0 / mixed[ch : ch + 1]
     position = mixed[ch + 1 : ch + 3] * inverse
@@ -344,12 +374,12 @@
 
     all_rs.wait_send()
     all_z.wait_send()
-    all_ag.wait_send()
+    ag_of(0).wait_send()
+    ag_of(1).wait_send()
     on_chip.wait_send()
-    for side in range(2):
-        part_copy(side).wait_send()
-    for copy in sib_copies:
-        copy.wait_send()
+    for slot in range(3):
+        for copy in part_copies(slot, sib, slot):
+            copy.wait_send()
     halo(0).wait_send()
     halo(1).wait_send()
     for r in range(1, n_tm):
@@ -378,9 +408,14 @@
         out = pl.pallas_call(
             functools.partial(kernel, dims),
             out_shape=pltpu.VMEM((2, n_q), F32),
-            in_specs=[pl.BlockSpec(memory_space=pl.ANY)] + [vmem] * 7,
+            in_specs=[pl.BlockSpec(memory_space=pl.ANY)] * 8,
             out_specs=vmem,
             scratch_shapes=[
+                pltpu.VMEM((3, n_q // 128, 128), jnp.int32),
+                pltpu.VMEM(decay.shape, F32),
+                pltpu.VMEM(taps.shape, F32),
+                pltpu.VMEM(pw.shape, BF16),
+                pltpu.VMEM(out_w.shape, F32),
                 pltpu.VMEM((n_q // 128, 128), jnp.int32),
                 pltpu.SMEM((n_q // 128, 128), jnp.int32),
                 pltpu.VMEM((n_pos, ch), BF16),
@@ -403,18 +438,17 @@
                 pltpu.VMEM((n_pos, q_blk), F32),
                 pltpu.VMEM((ch + 16, half), F32),
                 pltpu.VMEM((ch + 16, q_blk), F32),
-                pltpu.VMEM((3, ch + 16, q_blk), F32),
-                pltpu.VMEM((2, ch + 16, q_blk), F32),
-                pltpu.VMEM((ch, q_blk), SIB),
-                pltpu.VMEM((ch, q_blk), SIB),
-                pltpu.VMEM((16, q_blk), F32),
-                pltpu.VMEM((16, q_blk), F32),
+                pltpu.VMEM((ch + 8, q_blk), F32),
+                pltpu.VMEM((3, ch, q_blk), BF16),
+                pltpu.VMEM((3, ch, q_blk), BF16),
+                pltpu.VMEM((3, 16, q_blk), F32),
+                pltpu.VMEM((3, 16, q_blk), F32),
                 pltpu.VMEM((ch, q_blk), BF16),
                 pltpu.VMEM((2, ch, q_blk), BF16),
                 pltpu.VMEM((n_tm, 2, q_blk), F32),
                 pltpu.VMEM((n_tm, n_sp, 2, q_blk), F32),
-                dma((4,)), dma, dma, dma, dma, dma, dma, dma, dma, dma, dma, dma,
-                dma((2,)), dma((2,)), dma((2,)), dma((2,)), dma((2,)), dma((2,)),
+                dma((3,)), dma((4,)), dma((4,)), dma, dma, dma, dma, dma, dma((2,)), dma((2,)), dma, dma, dma, dma,
+                dma((3,)), dma((3,)), dma((3,)), dma((3,)), dma((2,)), dma((2,)),
                 dma((n_tm,)), dma((n_tm,)),
             ],
             compiler_params=pltpu.CompilerParams(collective_id=0, has_side_effects=True),

time: 39.6 us -> 38.2 us (0.965)
  Pallas kernels: 38.9 us -> 37.5 us
    pallas_call x1, Pallas kernels: 38.9 us -> 37.5 us  [local(): pl.pallas_call(functools.partial(kernel, dims), out_shape=pltpu.VMEM((2,...]
where the time goes in v5:
time: 38.2 us; the launch traced here: 38.1 us
  Pallas kernels  37.5 us (98%)
  local copies, waits for them, and re-layouts  0.6 us (2%)
    pallas_call x1, Pallas kernels, local(): pl.pallas_call(functools.partial(kernel, dims), out_shape=pltpu.VMEM((2,...  37.5 us

profile of v5, /device:TPU:1, one launch (start us, length us, event | category | flops | bytes accessed | tf_op | source)
XLA Modules:
  0.0 38.1 jit_solution(5731765637492454617)
XLA Ops:
  0.0 37.5 %shard_map.82 = f32[2,512]{1,0:T(2,128)S(1)} custom-call(bf16[7680,128]{1,0:T(8,128)(2,1)} %bitcast.6, s32[4,128]{1,0:T(4,128)} %bitcast.7, s32[4,128]{1,0:T(4,128)} %bitcast.8, s32[4,128]{1,0:T(4,128)} %bitcast.9, f32[1,128]{1,0:T(1,128)} %decay_hbm.1, f32[3,128]{1,0:T(4,128)} %taps_hbm.1, bf16[128,128]{1,0:T(8,128)(2,1)} %pw_hbm.1, f32[2,128]{1,0:T(2,128)} %out_w_hbm.1), custom_call_target="tpu_custom_call" | custom-call | tf_op jit(solution)/shard_map/pallas_call | solution.py:408
  37.5 0.6 %copy.10 = f32[1,2,512]{2,1,0:T(2,128)} copy(f32[1,2,512]{2,1,0:T(2,128)S(1)} %bitcast.5) | data formatting | bytes 8192

commit v6 on v5

--- a/solution.py
+++ b/solution.py
@@ -109,26 +109,21 @@
                     device_id={"tm": z * 2 + c, "space": block}, device_id_type=MESH,
                 ).start()
 
-    order = far_first(n_sp) + [0]
-    for i, k in enumerate(order):
+    @pl.loop(0, n_sp)
+    def _(i):
+        k = jnp.where(i == 0, 2, jnp.where(i == 1, 1, jnp.where(i == 2, 3, 0)))
         block = lax.rem(y + k, n_sp)
         first = pl.multiple_of(block * q_blk, q_blk)
-
-        @pl.loop(0, q_blk // 16)
-        def _(j):
-            for u in range(16):
-                at = rows_s[block, j * 16 + u]
-                contrib32[pl.ds(first + j * 16 + u, 1), :] = keys32[pl.ds(at, 1), :]
-
+        for u in range(q_blk):
+            at = rows_s[block, u]
+            contrib32[pl.ds(first + u, 1), :] = keys32[pl.ds(at, 1), :]
         contrib[pl.ds(block * 2, 2)] = (
             contrib32[pl.ds(first, q_blk), :].reshape(2, q_blk // 2, ch).astype(BF16)
         )
-        if i == 0:
-            pl.semaphore_wait(barrier, n_tm - 1 + plane - 2)
-            for past in order[:i]:
-                rs_sends(past)
-        if i >= 0:
-            rs_sends(k)
+
+    pl.semaphore_wait(barrier, n_tm - 1 + plane - 2)
+    for k in far_first(n_sp) + [0]:
+        rs_sends(k)
 
     for copy in smalls:
         copy.wait()
@@ -259,8 +254,8 @@
 
     def hand_over(slot, to, there, sums, top):
         feats[slot] = sums[:ch].astype(BF16)
-        facts[slot, pl.ds(0, 8), :] = sums[ch:]
-        facts[slot, pl.ds(8, 8), :] = jnp.broadcast_to(top, (8, q_blk))
+        spare = lax.broadcasted_iota(jnp.int32, (8, q_blk), 0) == 3
+        facts[slot] = jnp.where(spare, top, sums[ch:])
         for copy in part_copies(slot, to, there):
             copy.start()
 
@@ -293,8 +288,8 @@
         for copy in part_copies(slot, sib, slot):
             copy.wait_recv()
     for slot in range(3):
-        sums = jnp.concatenate([feats_in[slot].astype(F32), facts_in[slot, pl.ds(0, 8), :]], axis=0)
-        parts.append((sums, facts_in[slot, pl.ds(8, 1), :]))
+        sums = jnp.concatenate([feats_in[slot].astype(F32), facts_in[slot]], axis=0)
+        parts.append((sums, facts_in[slot, pl.ds(3, 1), :]))
     best = functools.reduce(jnp.maximum, [top for _, top in parts])
     mixed = None
     for sums, top in parts:
@@ -441,8 +436,8 @@
                 pltpu.VMEM((ch + 8, q_blk), F32),
                 pltpu.VMEM((3, ch, q_blk), BF16),
                 pltpu.VMEM((3, ch, q_blk), BF16),
-                pltpu.VMEM((3, 16, q_blk), F32),
-                pltpu.VMEM((3, 16, q_blk), F32),
+                pltpu.VMEM((3, 8, q_blk), F32),
+                pltpu.VMEM((3, 8, q_blk), F32),
                 pltpu.VMEM((ch, q_blk), BF16),
                 pltpu.VMEM((2, ch, q_blk), BF16),
                 pltpu.VMEM((n_tm, 2, q_blk), F32),

time: 38.2 us -> 37.7 us (0.987)
  Pallas kernels: 37.5 us -> 37 us
    pallas_call x1, Pallas kernels: 37.5 us -> 37 us  [local(): pl.pallas_call(functools.partial(kernel, dims), out_shape=pltpu.VMEM((2,...]
where the time goes in v6:
time: 37.7 us; the launch traced here: 37.6 us
  Pallas kernels  37 us (98%)
  local copies, waits for them, and re-layouts  0.6 us (2%)
    pallas_call x1, Pallas kernels, local(): pl.pallas_call(functools.partial(kernel, dims), out_shape=pltpu.VMEM((2,...  37 us

profile of v6, /device:TPU:1, one launch (start us, length us, event | category | flops | bytes accessed | tf_op | source)
XLA Modules:
  0.0 37.6 jit_solution(5645774021834879183)
XLA Ops:
  0.0 37.0 %shard_map.82 = f32[2,512]{1,0:T(2,128)S(1)} custom-call(bf16[7680,128]{1,0:T(8,128)(2,1)} %bitcast.6, s32[4,128]{1,0:T(4,128)} %bitcast.7, s32[4,128]{1,0:T(4,128)} %bitcast.8, s32[4,128]{1,0:T(4,128)} %bitcast.9, f32[1,128]{1,0:T(1,128)} %decay_hbm.1, f32[3,128]{1,0:T(4,128)} %taps_hbm.1, bf16[128,128]{1,0:T(8,128)(2,1)} %pw_hbm.1, f32[2,128]{1,0:T(2,128)} %out_w_hbm.1), custom_call_target="tpu_custom_call" | custom-call | tf_op jit(solution)/shard_map/pallas_call | solution.py:403
  37.0 0.6 %copy.10 = f32[1,2,512]{2,1,0:T(2,128)} copy(f32[1,2,512]{2,1,0:T(2,128)S(1)} %bitcast.5) | data formatting | bytes 8192

commit v7 on v6

--- a/solution.py
+++ b/solution.py
@@ -253,9 +253,12 @@
     top_sib = jnp.max(top_sib, axis=0, keepdims=True)
 
     def hand_over(slot, to, there, sums, top):
-        feats[slot] = sums[:ch].astype(BF16)
+        most = jnp.max(jnp.abs(sums[:ch]), axis=0, keepdims=True)
+        grain = jnp.maximum(most, 1e-30) * (1.0 / 32000.0)
+        feats[slot] = jnp.round(sums[:ch] * (1.0 / grain)).astype(jnp.int32).astype(jnp.int16)
         spare = lax.broadcasted_iota(jnp.int32, (8, q_blk), 0) == 3
-        facts[slot] = jnp.where(spare, top, sums[ch:])
+        spare_2 = lax.broadcasted_iota(jnp.int32, (8, q_blk), 0) == 4
+        facts[slot] = jnp.where(spare, top, jnp.where(spare_2, grain, sums[ch:]))
         for copy in part_copies(slot, to, there):
             copy.start()
 
@@ -288,7 +291,7 @@
         for copy in part_copies(slot, sib, slot):
             copy.wait_recv()
     for slot in range(3):
-        sums = jnp.concatenate([feats_in[slot].astype(F32), facts_in[slot]], axis=0)
+        sums = jnp.concatenate([feats_in[slot].astype(jnp.int32).astype(F32) * facts_in[slot, pl.ds(4, 1), :], facts_in[slot]], axis=0)
         parts.append((sums, facts_in[slot, pl.ds(3, 1), :]))
     best = functools.reduce(jnp.maximum, [top for _, top in parts])
     mixed = None
@@ -434,8 +437,8 @@
                 pltpu.VMEM((ch + 16, half), F32),
                 pltpu.VMEM((ch + 16, q_blk), F32),
                 pltpu.VMEM((ch + 8, q_blk), F32),
-                pltpu.VMEM((3, ch, q_blk), BF16),
-                pltpu.VMEM((3, ch, q_blk), BF16),
+                pltpu.VMEM((3, ch, q_blk), jnp.int16),
+                pltpu.VMEM((3, ch, q_blk), jnp.int16),
                 pltpu.VMEM((3, 8, q_blk), F32),
                 pltpu.VMEM((3, 8, q_blk), F32),
                 pltpu.VMEM((ch, q_blk), BF16),

time: 37.7 us -> 37.8 us (level)
  no operation moved by 1% of the time
where the time goes in v7:
time: 37.8 us; the launch traced here: 37.7 us
  Pallas kernels  37 us (98%)
  local copies, waits for them, and re-layouts  0.6 us (2%)
    pallas_call x1, Pallas kernels, local(): pl.pallas_call(functools.partial(kernel, dims), out_shape=pltpu.VMEM((2,...  37 us

profile of v7, /device:TPU:1, one launch (start us, length us, event | category | flops | bytes accessed | tf_op | source)
XLA Modules:
  0.0 37.7 jit_solution(12885845302066202311)
XLA Ops:
  0.0 37.0 %shard_map.82 = f32[2,512]{1,0:T(2,128)S(1)} custom-call(bf16[7680,128]{1,0:T(8,128)(2,1)} %bitcast.6, s32[4,128]{1,0:T(4,128)} %bitcast.7, s32[4,128]{1,0:T(4,128)} %bitcast.8, s32[4,128]{1,0:T(4,128)} %bitcast.9, f32[1,128]{1,0:T(1,128)} %decay_hbm.1, f32[3,128]{1,0:T(4,128)} %taps_hbm.1, bf16[128,128]{1,0:T(8,128)(2,1)} %pw_hbm.1, f32[2,128]{1,0:T(2,128)} %out_w_hbm.1), custom_call_target="tpu_custom_call" | custom-call | tf_op jit(solution)/shard_map/pallas_call | solution.py:406
  37.1 0.6 %copy.10 = f32[1,2,512]{2,1,0:T(2,128)} copy(f32[1,2,512]{2,1,0:T(2,128)S(1)} %bitcast.5) | data formatting | bytes 8192

commit v8 on v7

--- a/solution.py
+++ b/solution.py
@@ -314,12 +314,20 @@
             device_id={"tm": to}, device_id_type=MESH,
         )
 
-    halo(0).start()
-    halo(1).start()
+    for side, there in ((0, t < n_tm - 1), (1, t > 0)):
+
+        @pl.when(there)
+        def _():
+            halo(side).start()
+
     att = att.astype(F32)
     mid = att * tap_cols[1]
-    halo(0).wait_recv()
-    halo(1).wait_recv()
+    for side, there in ((0, t > 0), (1, t < n_tm - 1)):
+
+        @pl.when(there)
+        def _():
+            halo(side).wait_recv()
+
     before = jnp.where(t > 0, att_in[0].astype(F32), 0.0)
     after = jnp.where(t < n_tm - 1, att_in[1].astype(F32), 0.0)
     depth = tap_cols[0] * before + mid + tap_cols[2] * after
@@ -378,8 +386,12 @@
     for slot in range(3):
         for copy in part_copies(slot, sib, slot):
             copy.wait_send()
-    halo(0).wait_send()
-    halo(1).wait_send()
+    for side, there in ((0, t < n_tm - 1), (1, t > 0)):
+
+        @pl.when(there)
+        def _():
+            halo(side).wait_send()
+
     for r in range(1, n_tm):
 
         @pl.when(t + r < n_tm)

time: 37.8 us -> 37.8 us (level)
  no operation moved by 1% of the time
where the time goes in v8:
time: 37.8 us; the launch traced here: 37.7 us
  Pallas kernels  37.1 us (98%)
  local copies, waits for them, and re-layouts  0.6 us (2%)
    pallas_call x1, Pallas kernels, local(): pl.pallas_call(functools.partial(kernel, dims), out_shape=pltpu.VMEM((2,...  37.1 us

profile of v8, /device:TPU:1, one launch (start us, length us, event | category | flops | bytes accessed | tf_op | source)
XLA Modules:
  0.0 37.7 jit_solution(7366798675887864414)
XLA Ops:
  0.0 37.1 %shard_map.82 = f32[2,512]{1,0:T(2,128)S(1)} custom-call(bf16[7680,128]{1,0:T(8,128)(2,1)} %bitcast.6, s32[4,128]{1,0:T(4,128)} %bitcast.7, s32[4,128]{1,0:T(4,128)} %bitcast.8, s32[4,128]{1,0:T(4,128)} %bitcast.9, f32[1,128]{1,0:T(1,128)} %decay_hbm.1, f32[3,128]{1,0:T(4,128)} %taps_hbm.1, bf16[128,128]{1,0:T(8,128)(2,1)} %pw_hbm.1, f32[2,128]{1,0:T(2,128)} %out_w_hbm.1), custom_call_target="tpu_custom_call" | custom-call | tf_op jit(solution)/shard_map/pallas_call | solution.py:418
  37.1 0.6 %copy.10 = f32[1,2,512]{2,1,0:T(2,128)} copy(f32[1,2,512]{2,1,0:T(2,128)S(1)} %bitcast.5) | data formatting | bytes 8192
